TPU v7x, 128 devices: a whole 4x4x4 slice. The times are simulated.
128 devices in a mesh: seq: 32 (over x, y_lo, z), ch: 4 (over y_hi, core).
Axes of the slice: x: 4, y: 4 (y_hi: 2, y_lo: 2; y = y_hi * 2 + y_lo), z: 4, core: 2. Of those that a mesh axis runs over, the one named last changes fastest.
Arguments:
- query_proj: bfloat16 [4096, 4096], P('seq', 'ch'), may hold values from -6 to 6
- key_proj: bfloat16 [4096, 4096], P('seq', 'ch'), may hold values from -6 to 6
- value_proj: bfloat16 [4096, 4096], P('seq', 'ch'), may hold values from -6 to 6
- feat_weight: float32 [3, 3, 4096], P(None, None, 'ch'), may hold values from -3.5 to 3.5
- long_filter: float32 [4096, 4096], P('seq', 'ch'), may hold values from -2 to 2, as said below
- skip_gain: float32 [4096], P('ch'), may hold values from 0.5 to 1.5
- out_weight: bfloat16 [4096, 4096], P(None, 'ch'), may hold values from -0.09375 to 0.09375
Outputs:
- output: bfloat16 [4096, 4096], P('seq', 'ch')
Inputs may be any that keep to these rules, and one draw needn't show every extreme that they name: `long_filter`: taps of the long filters.
All inputs are finite; a program needn't handle non-finite values.
Results may differ from a plain program's by a relative error of at most 0.0049.
Values may be sent and summed in bfloat16 or wider, within the bound.
A program may use at most 128 MiB of HBM per device.

v0:
```python
import math

import jax
import jax.numpy as jnp
from jax import lax
from jax.sharding import PartitionSpec as P

exact_mode = lax.Precision.HIGHEST


def swapped(value, axis, bit):
    mask = 2**bit
    pairs = [(source, source ^ mask) for source in range(lax.axis_size(axis))]
    return lax.ppermute(value, axis, pairs)


def passed_along(value, axis, steps):
    count = lax.axis_size(axis)
    first, last = (max(0, -steps), min(count, count - steps))
    return lax.ppermute(value, axis, [(source, source + steps) for source in range(first, last)])


def rotate(real_part, imag_part, cosine, sine_value, direction):
    return (
        real_part * cosine - direction * imag_part * sine_value,
        imag_part * cosine + direction * real_part * sine_value,
    )


def row_transform(spectrum, direction):
    length = spectrum.shape[2]
    counter = jnp.arange(length, dtype=jnp.int32)
    phases = counter[:, None] * counter[None, :] % length
    angles = phases.astype(jnp.float32) * (2.0 * math.pi / length)
    cos_table = jnp.cos(angles)
    sin_table = jnp.sin(angles)

    def product_with(matrix, values):
        return jnp.einsum("kj,ejc->ekc", matrix, values, precision=exact_mode)

    real_part = product_with(cos_table, spectrum[0]) - direction * product_with(
        sin_table, spectrum[1]
    )
    imag_part = product_with(cos_table, spectrum[1]) + direction * product_with(
        sin_table, spectrum[0]
    )
    return jnp.stack([real_part, imag_part])


def twiddle_rows(spectrum, frequencies, total_len, direction):
    length = spectrum.shape[2]
    token_places = jnp.arange(length, dtype=jnp.int32)
    phases = frequencies[:, None] * token_places[None, :] % total_len
    angles = phases.astype(jnp.float32) * (2.0 * math.pi / total_len)
    cosine = jnp.cos(angles)[:, :, None]
    sine_value = jnp.sin(angles)[:, :, None]
    real_part, imag_part = rotate(spectrum[0], spectrum[1], cosine, sine_value, direction)
    return jnp.stack([real_part, imag_part])


def lift_pair(signal, cosine, sine_value):
    real_part = jnp.stack([signal, signal * cosine])
    imag_part = jnp.stack([jnp.zeros_like(signal), -signal * sine_value])
    return jnp.stack([real_part, imag_part])


def pair_forward(gated, long_filter):
    devices = lax.axis_size("seq")
    position = lax.axis_index("seq")
    row_count = gated.shape[0]
    total_len = 2 * row_count * devices
    bit_count = devices.bit_length() - 1
    base_angle = position.astype(jnp.float32) * (math.pi / devices)
    signals = (
        lift_pair(gated, jnp.cos(base_angle), jnp.sin(base_angle)),
        lift_pair(long_filter, jnp.cos(base_angle), jnp.sin(base_angle)),
    )
    for section_bit in reversed(range(bit_count)):
        half_span = 1 << section_bit
        partners = swapped(signals, "seq", section_bit)
        upper_bit = position // half_span % 2
        sign_factor = (1 - 2 * upper_bit).astype(jnp.float32)
        turn_angle = (upper_bit * (position % half_span)).astype(jnp.float32) * (
            math.pi / half_span
        )
        cosine = jnp.cos(turn_angle)
        sine_value = jnp.sin(turn_angle)
        updated = []
        for own_part, peer_part in zip(signals, partners):
            combined = peer_part + sign_factor * own_part
            real_part, imag_part = rotate(combined[0], combined[1], cosine, sine_value, -1.0)
            updated.append(jnp.stack([real_part, imag_part]))
        signals = tuple(updated)
    flipped = jnp.zeros((), jnp.int32)
    for section_bit in range(bit_count):
        flipped = flipped + position // (1 << section_bit) % 2 * (1 << bit_count - 1 - section_bit)
    frequencies = 2 * flipped + jnp.arange(2, dtype=jnp.int32)
    spectra = tuple(
        (
            row_transform(twiddle_rows(member, frequencies, total_len, -1.0), -1.0)
            for member in signals
        )
    )
    return (spectra, frequencies)


def pair_inverse(spectrum):
    devices = lax.axis_size("seq")
    position = lax.axis_index("seq")
    row_count = spectrum.shape[2]
    bit_count = devices.bit_length() - 1
    for section_bit in range(bit_count):
        half_span = 1 << section_bit
        partner = swapped(spectrum, "seq", section_bit)
        upper_bit = position // half_span % 2
        sign_factor = (1 - 2 * upper_bit).astype(jnp.float32)
        lower_part = jnp.where(upper_bit == 1, partner, spectrum)
        upper_part = jnp.where(upper_bit == 1, spectrum, partner)
        turn_angle = (position % half_span).astype(jnp.float32) * (math.pi / half_span)
        real_part, imag_part = rotate(
            upper_part[0], upper_part[1], jnp.cos(turn_angle), jnp.sin(turn_angle), 1.0
        )
        spectrum = 0.5 * (lower_part + sign_factor * jnp.stack([real_part, imag_part]))
    base_angle = position.astype(jnp.float32) * (math.pi / devices)
    summed = (
        spectrum[0, 0] + jnp.cos(base_angle) * spectrum[0, 1] - jnp.sin(base_angle) * spectrum[1, 1]
    )
    return summed / (2.0 * row_count)


def long_convolution(gated, long_filter):
    row_count, columns = gated.shape
    groups = long_filter.shape[1]
    total_len = 2 * row_count * lax.axis_size("seq")
    spectra, frequencies = pair_forward(gated, long_filter)
    signal_spec = spectra[0].reshape(2, 2, row_count, groups, columns // groups)
    filter_spec = spectra[1][..., None]
    real_part = signal_spec[0] * filter_spec[0] - signal_spec[1] * filter_spec[1]
    imag_part = signal_spec[0] * filter_spec[1] + signal_spec[1] * filter_spec[0]
    product = jnp.stack([real_part, imag_part]).reshape(2, 2, row_count, columns)
    returned = twiddle_rows(row_transform(product, 1.0), frequencies, total_len, 1.0)
    return pair_inverse(returned)


def featurize(signal, prior_rows, tap_weights):
    reach_rows = prior_rows.shape[0]
    row_count = signal.shape[0]
    extended = jnp.concatenate([prior_rows, signal], axis=0).astype(jnp.float32)
    result = jnp.zeros(signal.shape, jnp.float32)
    for tap_lag in range(reach_rows + 1):
        result = (
            result
            + tap_weights[tap_lag][None, :]
            * extended[reach_rows - tap_lag : reach_rows - tap_lag + row_count]
        )
    return result


def shards(query_proj, key_proj, value_proj, feat_weight, long_filter, skip_gain, out_weight):
    row_count = query_proj.shape[0]
    reach_rows = feat_weight.shape[1] - 1
    tail_block = jnp.stack(
        [
            query_proj[row_count - reach_rows :],
            key_proj[row_count - reach_rows :],
            value_proj[row_count - reach_rows :],
        ]
    )
    prior_block = passed_along(tail_block, "seq", 1)
    query_feat = featurize(query_proj, prior_block[0], feat_weight[0])
    key_feat = featurize(key_proj, prior_block[1], feat_weight[1])
    value_feat = featurize(value_proj, prior_block[2], feat_weight[2])
    gated = key_feat * value_feat
    convolved = long_convolution(gated, long_filter)
    mixed = (query_feat * (convolved + skip_gain[None, :] * gated)).astype(jnp.bfloat16)
    output = jnp.dot(
        lax.all_gather(mixed, "ch", axis=1, tiled=True),
        out_weight,
        preferred_element_type=jnp.float32,
    )
    return output.astype(jnp.bfloat16)


def solution(mesh):
    placed = (
        P("seq", "ch"),
        P("seq", "ch"),
        P("seq", "ch"),
        P(None, None, "ch"),
        P("seq", "ch"),
        P("ch"),
        P(None, "ch"),
    )
    return jax.shard_map(
        shards, mesh=mesh, in_specs=placed, out_specs=P("seq", "ch"), check_vma=False
    )
```

profile of v0, /device:TPU:1, one launch (start us, length us, event | category | flops | bytes accessed | tf_op | source)
XLA Modules:
  0.0 689.7 jit_solution(12364181018840660812)
XLA Ops:
  9.7 3.6 collective-permute-start.6
  13.3 3.5 collective-permute-start
  18.6 1.5 multiply_bitcast_fusion.3
  21.0 1.7 pad_maximum_fusion
  22.7 48.6 %collective-permute-start.1 = (f32[2,2,128,1024]{2,3,1,0:T(8,128)}, f32[2,2,128,1024]{2,3,1,0:T(8,128)}, u32[]{:S(2)}, u32[]{:S(2)}) collective-permute-start(f32[2,2,128,1024]{2,3,1,0:T(8,128)} %pad_maximum_fusion), channel_id=1, source_target_pairs={{0,64},{4,68},{8,72},{12,76},{16,80},{20,84},{24,88},{28,92},{32,9... | collective-permute-start | bytes 6291464 | tf_op jit(solution)/shard_map/ppermute | solution.py:14
  71.4 1.8 multiply_add_fusion.4
  75.0 41.1 %collective-permute-done.1 = f32[2,2,128,1024]{2,3,1,0:T(8,128)} collective-permute-done((f32[2,2,128,1024]{2,3,1,0:T(8,128)}, f32[2,2,128,1024]{2,3,1,0:T(8,128)}, u32[]{:S(2)}, u32[]{:S(2)}) %collective-permute-start.1) | collective-permute-done | bytes 2097184 | tf_op jit(solution)/shard_map/ppermute | solution.py:14
  116.1 1.9 multiply_add_fusion.9
  118.2 1.7 pad_maximum_fusion.1
  120.6 39.4 %collective-permute-done.7 = f32[2,2,128,1024]{2,3,1,0:T(8,128)} collective-permute-done((f32[2,2,128,1024]{2,3,1,0:T(8,128)}, f32[2,2,128,1024]{2,3,1,0:T(8,128)}, u32[]{:S(2)}, u32[]{:S(2)}) %collective-permute-start.7) | collective-permute-done | bytes 2097184 | tf_op jit(solution)/shard_map/ppermute | solution.py:14
  160.0 1.8 multiply_add_fusion.3
  163.5 41.4 %collective-permute-done.2 = f32[2,2,128,1024]{2,3,1,0:T(8,128)} collective-permute-done((f32[2,2,128,1024]{2,3,1,0:T(8,128)}, f32[2,2,128,1024]{2,3,1,0:T(8,128)}, u32[]{:S(2)}, u32[]{:S(2)}) %collective-permute-start.2) | collective-permute-done | bytes 2097184 | tf_op jit(solution)/shard_map/ppermute | solution.py:14
  204.9 1.9 multiply_add_fusion.8
  207.1 1.6 pad_maximum_fusion.2
  209.3 1.8 multiply_add_fusion.2
  211.4 1.5 pad_maximum_fusion.8
  213.0 41.3 %collective-permute-done.3 = f32[2,2,128,1024]{2,3,1,0:T(8,128)} collective-permute-done((f32[2,2,128,1024]{2,3,1,0:T(8,128)}, f32[2,2,128,1024]{2,3,1,0:T(8,128)}, u32[]{:S(2)}, u32[]{:S(2)}) %collective-permute-start.3) | collective-permute-done | bytes 2097184 | tf_op jit(solution)/shard_map/ppermute | solution.py:14
  254.3 1.9 multiply_add_fusion.7
  256.4 1.5 pad_maximum_fusion.3
  259.5 2.1 multiply_add_fusion.1
  261.8 1.7 pad_maximum_fusion.9
  263.5 40.3 %collective-permute-done.4 = f32[2,2,128,1024]{2,3,1,0:T(8,128)} collective-permute-done((f32[2,2,128,1024]{2,3,1,0:T(8,128)}, f32[2,2,128,1024]{2,3,1,0:T(8,128)}, u32[]{:S(2)}, u32[]{:S(2)}) %collective-permute-start.4) | collective-permute-done | bytes 2097184 | tf_op jit(solution)/shard_map/ppermute | solution.py:14
  303.8 1.8 multiply_add_fusion.6
  306.7 38.7 %collective-permute-done.10 = f32[2,2,128,1024]{2,3,1,0:T(8,128)} collective-permute-done((f32[2,2,128,1024]{2,3,1,0:T(8,128)}, f32[2,2,128,1024]{2,3,1,0:T(8,128)}, u32[]{:S(2)}, u32[]{:S(2)}) %collective-permute-start.10) | collective-permute-done | bytes 2097184 | tf_op jit(solution)/shard_map/ppermute | solution.py:14
  345.3 1.9 multiply_add_fusion
  352.4 37.7 %collective-permute-done.5 = f32[2,2,128,1024]{2,3,1,0:T(8,128)S(1)} collective-permute-done((f32[2,2,128,1024]{2,3,1,0:T(8,128)S(1)}, f32[2,2,128,1024]{2,3,1,0:T(8,128)S(1)}, u32[]{:S(2)}, u32[]{:S(2)}) %collective-permute-start.5) | collective-permute-done | bytes 2097184 | tf_op jit(solution)/shard_map/ppermute | solution.py:14
  394.3 1.5 multiply_add_fusion.15
  401.1 1.5 pad_maximum_fusion.10
  402.6 2.2 collective-permute-start.11
  404.8 42.6 %collective-permute-done.11 = f32[2,2,128,1024]{2,3,1,0:T(8,128)} collective-permute-done((f32[2,2,128,1024]{2,3,1,0:T(8,128)}, f32[2,2,128,1024]{2,3,1,0:T(8,128)}, u32[]{:S(2)}, u32[]{:S(2)}) %collective-permute-start.11) | collective-permute-done | bytes 2097184 | tf_op jit(solution)/shard_map/ppermute | solution.py:14
  447.4 1.8 broadcast_select_fusion
  449.4 1.7 fusion.1
  451.0 2.4 collective-permute-start.12
  453.6 42.1 %collective-permute-done.12 = f32[2,2,128,1024]{2,3,1,0:T(8,128)} collective-permute-done((f32[2,2,128,1024]{2,3,1,0:T(8,128)}, f32[2,2,128,1024]{2,3,1,0:T(8,128)}, u32[]{:S(2)}, u32[]{:S(2)}) %collective-permute-start.12) | collective-permute-done | bytes 2097184 | tf_op jit(solution)/shard_map/ppermute | solution.py:14
  495.7 2.2 broadcast_select_fusion.1
  499.2 2.0 fusion.3
  501.2 5.8 collective-permute-start.13
  507.2 42.4 %collective-permute-done.13 = f32[2,2,128,1024]{2,3,1,0:T(8,128)S(1)} collective-permute-done((f32[2,2,128,1024]{2,3,1,0:T(8,128)}, f32[2,2,128,1024]{2,3,1,0:T(8,128)S(1)}, u32[]{:S(2)}, u32[]{:S(2)}) %collective-permute-start.13) | collective-permute-done | bytes 2097184 | tf_op jit(solution)/shard_map/ppermute | solution.py:14
  551.1 1.9 fusion.5
  553.0 2.3 collective-permute-start.14
  555.5 41.7 %collective-permute-done.14 = f32[2,2,128,1024]{2,3,1,0:T(8,128)} collective-permute-done((f32[2,2,128,1024]{2,3,1,0:T(8,128)S(1)}, f32[2,2,128,1024]{2,3,1,0:T(8,128)}, u32[]{:S(2)}, u32[]{:S(2)}) %collective-permute-start.14) | collective-permute-done | bytes 2097184 | tf_op jit(solution)/shard_map/ppermute | solution.py:14
  597.2 1.8 broadcast_select_fusion.3
  599.2 1.9 fusion.7
  603.4 42.0 %collective-permute-done.15 = f32[2,2,128,1024]{2,3,1,0:T(8,128)} collective-permute-done((f32[2,2,128,1024]{2,3,1,0:T(8,128)S(1)}, f32[2,2,128,1024]{2,3,1,0:T(8,128)}, u32[]{:S(2)}, u32[]{:S(2)}) %collective-permute-start.15) | collective-permute-done | bytes 2097184 | tf_op jit(solution)/shard_map/ppermute | solution.py:14
  645.4 1.8 broadcast_select_fusion.4
  648.4 1.6 fusion.25
  650.1 26.8 %all-gather.2.cloned.1.call-done = bf16[128,4096]{0,1:T(8,128)(2,1)} async-done(((bf16[128,1024]{0,1:T(8,128)(2,1)}), bf16[128,4096]{0,1:T(8,128)(2,1)}) %all-gather.2.cloned.1.call-update) | async-done | bytes 1048592 | tf_op jit(solution)/shard_map/all_gather | solution.py:177
  676.9 5.7 convolution_convert_fusion
  (114 shorter events, 34.6 us)
Async XLA Ops:
  6.5 670.4 %all-gather.2.cloned.1.call-start = ((), (), s32[]{:S(2)}) async-start(), calls=%async_computation | async-start | bytes 1310720 | tf_op jit(solution)/shard_map/all_gather | solution.py:177
  8.2 5.1 copy-start.17
  8.2 5.1 copy-start.18
  8.2 5.1 copy-start.19
  8.2 8.7 %copy-start.20 = (f32[3,3,1024]{2,1,0:T(4,128)S(1)}, f32[3,3,1024]{2,1,0:T(4,128)}, u32[]{:S(2)}) copy-start(f32[3,3,1024]{2,1,0:T(4,128)} %param.10) | copy-start | bytes 110596
  9.7 61.7 %collective-permute-start.6 = (f32[2,2,128,1024]{2,3,1,0:T(8,128)}, f32[2,2,128,1024]{2,3,1,0:T(8,128)}, u32[]{:S(2)}, u32[]{:S(2)}) collective-permute-start(f32[2,2,128,1024]{2,3,1,0:T(8,128)} %pad_maximum_fusion.5), channel_id=1, source_target_pairs={{0,64},{4,68},{8,72},{12,76},{16,80},{20,84},{24,88},{28,92},{32,9... | collective-permute-start | bytes 6291464 | tf_op jit(solution)/shard_map/ppermute | solution.py:14
  13.3 4.4 collective-permute-start
  20.2 0.8 copy-start.15
  21.0 1.7 copy-start.12
  22.7 93.4 %collective-permute-start.1 = (f32[2,2,128,1024]{2,3,1,0:T(8,128)}, f32[2,2,128,1024]{2,3,1,0:T(8,128)}, u32[]{:S(2)}, u32[]{:S(2)}) collective-permute-start(f32[2,2,128,1024]{2,3,1,0:T(8,128)} %pad_maximum_fusion), channel_id=1, source_target_pairs={{0,64},{4,68},{8,72},{12,76},{16,80},{20,84},{24,88},{28,92},{32,9... | collective-permute-start | bytes 6291464 | tf_op jit(solution)/shard_map/ppermute | solution.py:14
  73.5 42.6 %copy-start.13 = (f32[1,2,128,1024]{2,3,1,0:T(8,128)S(1)}, f32[1,2,128,1024]{2,3,1,0:T(8,128)}, u32[]{:S(2)}) copy-start(f32[1,2,128,1024]{2,3,1,0:T(8,128)} %copy-done.12) | copy-start | bytes 3145732
  75.0 85.0 %collective-permute-start.7 = (f32[2,2,128,1024]{2,3,1,0:T(8,128)}, f32[2,2,128,1024]{2,3,1,0:T(8,128)}, u32[]{:S(2)}, u32[]{:S(2)}) collective-permute-start(f32[2,2,128,1024]{2,3,1,0:T(8,128)} %pad_maximum_fusion.6), channel_id=1, source_target_pairs={{0,32},{4,36},{8,40},{12,44},{16,48},{20,52},{24,56},{28,60},{32,0... | collective-permute-start | bytes 6291464 | tf_op jit(solution)/shard_map/ppermute | solution.py:14
  118.2 1.7 copy-start.8
  119.9 85.1 %collective-permute-start.2 = (f32[2,2,128,1024]{2,3,1,0:T(8,128)}, f32[2,2,128,1024]{2,3,1,0:T(8,128)}, u32[]{:S(2)}, u32[]{:S(2)}) collective-permute-start(f32[2,2,128,1024]{2,3,1,0:T(8,128)} %pad_maximum_fusion.1), channel_id=1, source_target_pairs={{0,32},{4,36},{8,40},{12,44},{16,48},{20,52},{24,56},{28,60},{32,0... | collective-permute-start | bytes 6291464 | tf_op jit(solution)/shard_map/ppermute | solution.py:14
  162.0 42.9 %copy-start.9 = (f32[1,2,128,1024]{2,3,1,0:T(8,128)S(1)}, f32[1,2,128,1024]{2,3,1,0:T(8,128)}, u32[]{:S(2)}) copy-start(f32[1,2,128,1024]{2,3,1,0:T(8,128)} %copy-done.8) | copy-start | bytes 3145732
  163.5 45.8 %collective-permute-start.8 = (f32[2,2,128,1024]{2,3,1,0:T(8,128)}, f32[2,2,128,1024]{2,3,1,0:T(8,128)}, u32[]{:S(2)}, u32[]{:S(2)}) collective-permute-start(f32[2,2,128,1024]{2,3,1,0:T(8,128)} %pad_maximum_fusion.7), channel_id=1, source_target_pairs={{0,16},{4,20},{8,24},{12,28},{16,0},{20,4},{24,8},{28,12},{32,48},... | collective-permute-start | bytes 6291464 | tf_op jit(solution)/shard_map/ppermute | solution.py:14
  207.1 1.7 copy-start.4
  207.1 2.0 copy-start.6
  209.1 45.1 %collective-permute-start.3 = (f32[2,2,128,1024]{2,3,1,0:T(8,128)}, f32[2,2,128,1024]{2,3,1,0:T(8,128)}, u32[]{:S(2)}, u32[]{:S(2)}) collective-permute-start(f32[2,2,128,1024]{2,3,1,0:T(8,128)} %pad_maximum_fusion.2), channel_id=1, source_target_pairs={{0,16},{4,20},{8,24},{12,28},{16,0},{20,4},{24,8},{28,12},{32,48},... | collective-permute-start | bytes 6291464 | tf_op jit(solution)/shard_map/ppermute | solution.py:14
  211.4 1.7 copy-start.3
  211.4 42.9 %copy-start.5 = (f32[1,2,128,1024]{2,3,1,0:T(8,128)S(1)}, f32[1,2,128,1024]{2,3,1,0:T(8,128)}, u32[]{:S(2)}) copy-start(f32[1,2,128,1024]{2,3,1,0:T(8,128)} %copy-done.4) | copy-start | bytes 3145732
  211.4 42.9 %copy-start.7 = (f32[1,2,128,1024]{2,3,1,0:T(8,128)S(1)}, f32[1,2,128,1024]{2,3,1,0:T(8,128)}, u32[]{:S(2)}) copy-start(f32[1,2,128,1024]{2,3,1,0:T(8,128)} %copy-done.6) | copy-start | bytes 3145732
  213.0 46.4 %collective-permute-start.9 = (f32[2,2,128,1024]{2,3,1,0:T(8,128)}, f32[2,2,128,1024]{2,3,1,0:T(8,128)}, u32[]{:S(2)}, u32[]{:S(2)}) collective-permute-start(f32[2,2,128,1024]{2,3,1,0:T(8,128)} %pad_maximum_fusion.8), channel_id=1, source_target_pairs={{0,8},{4,12},{8,0},{12,4},{16,24},{20,28},{24,16},{28,20},{32,40},... | collective-permute-start | bytes 6291464 | tf_op jit(solution)/shard_map/ppermute | solution.py:14
  257.9 45.9 %collective-permute-start.4 = (f32[2,2,128,1024]{2,3,1,0:T(8,128)}, f32[2,2,128,1024]{2,3,1,0:T(8,128)}, u32[]{:S(2)}, u32[]{:S(2)}) collective-permute-start(f32[2,2,128,1024]{2,3,1,0:T(8,128)} %pad_maximum_fusion.3), channel_id=1, source_target_pairs={{0,8},{4,12},{8,0},{12,4},{16,24},{20,28},{24,16},{28,20},{32,40},... | collective-permute-start | bytes 6291464 | tf_op jit(solution)/shard_map/ppermute | solution.py:14
  261.8 1.7 copy-start.10
  263.5 81.8 %collective-permute-start.10 = (f32[2,2,128,1024]{2,3,1,0:T(8,128)}, f32[2,2,128,1024]{2,3,1,0:T(8,128)}, u32[]{:S(2)}, u32[]{:S(2)}) collective-permute-start(f32[2,2,128,1024]{2,3,1,0:T(8,128)} %pad_maximum_fusion.9), channel_id=1, source_target_pairs={{0,4},{4,0},{8,12},{12,8},{16,20},{20,16},{24,28},{28,24},{32,36},... | collective-permute-start | bytes 6291464 | tf_op jit(solution)/shard_map/ppermute | solution.py:14
  305.9 39.5 %copy-start.11 = (f32[1,2,128,1024]{2,3,1,0:T(8,128)S(1)}, f32[1,2,128,1024]{2,3,1,0:T(8,128)}, u32[]{:S(2)}) copy-start(f32[1,2,128,1024]{2,3,1,0:T(8,128)} %copy-done.10) | copy-start | bytes 3145732
  306.0 84.2 %collective-permute-start.5 = (f32[2,2,128,1024]{2,3,1,0:T(8,128)S(1)}, f32[2,2,128,1024]{2,3,1,0:T(8,128)S(1)}, u32[]{:S(2)}, u32[]{:S(2)}) collective-permute-start(f32[2,2,128,1024]{2,3,1,0:T(8,128)S(1)} %pad_maximum_fusion.4), channel_id=1, source_target_pairs={{0,4},{4,0},{8,12},{12,8},{16,20},{20,16},{24,28},{28,24},{32,36},... | collective-permute-start | bytes 6291464 | tf_op jit(solution)/shard_map/ppermute | solution.py:14
  402.6 44.8 %collective-permute-start.11 = (f32[2,2,128,1024]{2,3,1,0:T(8,128)}, f32[2,2,128,1024]{2,3,1,0:T(8,128)}, u32[]{:S(2)}, u32[]{:S(2)}) collective-permute-start(f32[2,2,128,1024]{2,3,1,0:T(8,128)} %pad_maximum_fusion.10), channel_id=1, source_target_pairs={{0,4},{4,0},{8,12},{12,8},{16,20},{20,16},{24,28},{28,24},{32,36},... | collective-permute-start | bytes 6291464 | tf_op jit(solution)/shard_map/ppermute | solution.py:14
  449.4 1.7 copy-start.1
  451.0 44.7 %collective-permute-start.12 = (f32[2,2,128,1024]{2,3,1,0:T(8,128)}, f32[2,2,128,1024]{2,3,1,0:T(8,128)}, u32[]{:S(2)}, u32[]{:S(2)}) collective-permute-start(f32[2,2,128,1024]{2,3,1,0:T(8,128)} %fusion.1), channel_id=1, source_target_pairs={{0,8},{4,12},{8,0},{12,4},{16,24},{20,28},{24,16},{28,20},{32,40},... | collective-permute-start | bytes 6291464 | tf_op jit(solution)/shard_map/ppermute | solution.py:14
  498.0 1.2 copy-start.2
  501.2 48.4 %collective-permute-start.13 = (f32[2,2,128,1024]{2,3,1,0:T(8,128)}, f32[2,2,128,1024]{2,3,1,0:T(8,128)S(1)}, u32[]{:S(2)}, u32[]{:S(2)}) collective-permute-start(f32[2,2,128,1024]{2,3,1,0:T(8,128)} %fusion.3), channel_id=1, source_target_pairs={{0,16},{4,20},{8,24},{12,28},{16,0},{20,4},{24,8},{28,12},{32,48},... | collective-permute-start | bytes 6291464 | tf_op jit(solution)/shard_map/ppermute | solution.py:14
  549.6 1.3 copy-start.14
  553.0 45.9 %copy-start = (f32[2,2,128,1024]{2,3,1,0:T(8,128)}, f32[2,2,128,1024]{2,3,1,0:T(8,128)S(1)}, u32[]{:S(2)}) copy-start(f32[2,2,128,1024]{2,3,1,0:T(8,128)S(1)} %fusion.5) | copy-start | bytes 6291460
  553.0 44.1 %collective-permute-start.14 = (f32[2,2,128,1024]{2,3,1,0:T(8,128)S(1)}, f32[2,2,128,1024]{2,3,1,0:T(8,128)}, u32[]{:S(2)}, u32[]{:S(2)}) collective-permute-start(f32[2,2,128,1024]{2,3,1,0:T(8,128)S(1)} %fusion.5), channel_id=1, source_target_pairs={{0,32},{4,36},{8,40},{12,44},{16,48},{20,52},{24,56},{28,60},{32,0... | collective-permute-start | bytes 6291464 | tf_op jit(solution)/shard_map/ppermute | solution.py:14
  601.1 44.2 %collective-permute-start.15 = (f32[2,2,128,1024]{2,3,1,0:T(8,128)S(1)}, f32[2,2,128,1024]{2,3,1,0:T(8,128)}, u32[]{:S(2)}, u32[]{:S(2)}) collective-permute-start(f32[2,2,128,1024]{2,3,1,0:T(8,128)S(1)} %fusion.7), channel_id=1, source_target_pairs={{0,64},{4,68},{8,72},{12,76},{16,80},{20,84},{24,88},{28,92},{32,9... | collective-permute-start | bytes 6291464 | tf_op jit(solution)/shard_map/ppermute | solution.py:14
  647.4 1.0 copy-start.16
  647.4 1.0 copy-start.21
Sparse Core Ops, SparseCore 0:
  650.2 26.6 all-gather.1
where the time goes:
time: 698 us; the launch traced here: 690 us
  waiting for transfers between devices  519 us (74%)
  starting transfers between devices  71 us (10%)
  other arithmetic  55.9 us (8%)
  matrix products  21.2 us (3%)
  between operations  15.7 us (2%)
    ppermute x15, waiting for transfers between devices, swapped(): return lax.ppermute(value, axis, pairs)  492 us
    ppermute x15, starting transfers between devices, swapped(): return lax.ppermute(value, axis, pairs)  67.5 us
    all_gather x1, waiting for transfers between devices, shards(): lax.all_gather(mixed, 'ch', axis=1, tiled=True)  26.8 us
    add x10, other arithmetic, pair_forward(): combined = peer_part + sign_factor * own_part  17 us
    dot_general x12, matrix products, product_with(): return jnp.einsum('kj,ejc->ekc', matrix, values, precision=exact_mode)  15.5 us
  transfers between devices with their start and end apart: 17, of which 15 were waited for; matrix products, arithmetic and copies ran while one was open for 6% of the time, Pallas kernels for 0%

commit v1 on v0

v1 whole, which is shorter than its diff:
```python
import functools

import jax
import jax.numpy as jnp
import numpy as np
from jax import lax
from jax.experimental import pallas as pl
from jax.experimental.pallas import tpu as pltpu
from jax.sharding import PartitionSpec as P

F32 = jnp.float32
BF16 = jnp.bfloat16
MESH = pl.DeviceIdType.MESH
BLOCKS = 32
LANES = 128
ROWS = 16
HALF_ROOT = float(np.sqrt(0.5))


def tables():
    lane = np.arange(LANES)
    theta = 2 * np.pi * (np.arange(BLOCKS)[:, None] + 0.25) * lane[None, :] / (BLOCKS * LANES)
    twiddle = np.stack([np.cos(theta), np.sin(theta)]).astype(np.float32)
    phase = 2 * np.pi * (lane[:, None] * lane[None, :] % LANES) / LANES
    c, s = np.cos(phase), np.sin(phase)
    forward = np.block([[c, -s], [s, c]])
    inverse = np.block([[c, s], [-s, c]]) / (BLOCKS * LANES)
    parts = []
    for matrix in (forward, inverse):
        high = matrix.astype(BF16)
        parts += [high, (matrix - high.astype(np.float64)).astype(BF16)]
    return jnp.asarray(twiddle), jnp.asarray(np.stack(parts))


def times(value, angle):
    re, im = value
    c, s = float(np.cos(angle)), float(np.sin(angle))
    if abs(angle) < 1e-12:
        return re, im
    return re * c - im * s, im * c + re * s


def fft4(x, sign):
    (ar, ai), (br, bi), (cr, ci), (dr, di) = x
    er, ei, fr, fi = ar + cr, ai + ci, ar - cr, ai - ci
    gr, gi, hr, hi = br + dr, bi + di, br - dr, bi - di
    if sign < 0:
        jr, ji = hi, -hr
    else:
        jr, ji = -hi, hr
    return [(er + gr, ei + gi), (fr + jr, fi + ji), (er - gr, ei - gi), (fr - jr, fi - ji)]


def fft8(x, sign):
    even = fft4(x[0::2], sign)
    odd = fft4(x[1::2], sign)
    o1r, o1i = odd[1]
    o2r, o2i = odd[2]
    o3r, o3i = odd[3]
    if sign < 0:
        odd[1] = ((o1r + o1i) * HALF_ROOT, (o1i - o1r) * HALF_ROOT)
        odd[2] = (o2i, -o2r)
        odd[3] = ((o3i - o3r) * HALF_ROOT, (-o3i - o3r) * HALF_ROOT)
    else:
        odd[1] = ((o1r - o1i) * HALF_ROOT, (o1i + o1r) * HALF_ROOT)
        odd[2] = (-o2i, o2r)
        odd[3] = ((-o3r - o3i) * HALF_ROOT, (o3r - o3i) * HALF_ROOT)
    low = [(e[0] + o[0], e[1] + o[1]) for e, o in zip(even, odd)]
    high = [(e[0] - o[0], e[1] - o[1]) for e, o in zip(even, odd)]
    return low + high


def store_split(high_ref, low_ref, index, value):
    high = value.astype(BF16)
    high_ref[index] = high
    low_ref[index] = (value - high.astype(F32)).astype(BF16)


def forward_blocks(source, half, mid, high_ref, low_ref, twiddle):
    for k2 in range(8):
        x = [source[k2 + 8 * k1, half].astype(F32) for k1 in range(4)]
        x0, x1, x2, x3 = x

        def real_times(value, angle):
            return value * float(np.cos(angle)), value * float(np.sin(angle))

        t1 = real_times(x1, -2 * np.pi / 16)
        t2 = real_times(x2, -2 * np.pi * 2 / 16)
        t3 = real_times(x3, -2 * np.pi * 3 / 16)
        er, ei, fr, fi = x0 + t2[0], t2[1], x0 - t2[0], -t2[1]
        gr, gi, hr, hi = t1[0] + t3[0], t1[1] + t3[1], t1[0] - t3[0], t1[1] - t3[1]
        results = [(er + gr, ei + gi), (fr + hi, fi - hr), (er - gr, ei - gi), (fr - hi, fi + hr)]
        for f1 in range(4):
            re, im = times(results[f1], -2 * np.pi * k2 * (0.25 + f1) / 32)
            mid[0, f1, k2] = re
            mid[1, f1, k2] = im
    for f1 in range(4):
        spectrum = fft8([(mid[0, f1, k2], mid[1, f1, k2]) for k2 in range(8)], -1)
        for f2 in range(8):
            f = f1 + 4 * f2
            c = twiddle[0, f : f + 1, :]
            s = twiddle[1, f : f + 1, :]
            re, im = spectrum[f2]
            rows = pl.ds(f * ROWS, ROWS)
            store_split(high_ref, low_ref, (rows, pl.ds(0, LANES)), re * c + im * s)
            store_split(high_ref, low_ref, (rows, pl.ds(LANES, LANES)), im * c - re * s)


def inverse_blocks(source, mid, out, half, twiddle):
    for f1 in range(4):
        values = []
        for f2 in range(8):
            f = f1 + 4 * f2
            c = twiddle[0, f : f + 1, :]
            s = twiddle[1, f : f + 1, :]
            re = source[pl.ds(f * ROWS, ROWS), pl.ds(0, LANES)]
            im = source[pl.ds(f * ROWS, ROWS), pl.ds(LANES, LANES)]
            values.append((re * c - im * s, im * c + re * s))
        spectrum = fft8(values, 1)
        for k2 in range(8):
            re, im = times(spectrum[k2], 2 * np.pi * k2 * (0.25 + f1) / 32)
            mid[0, f1, k2] = re
            mid[1, f1, k2] = im
    for k2 in range(8):
        u = fft4([(mid[0, f1, k2], mid[1, f1, k2]) for f1 in range(4)], 1)
        for k1 in range(4):
            angle = 2 * np.pi * k1 / 16
            re, im = u[k1]
            y = re if k1 == 0 else re * float(np.cos(angle)) - im * float(np.sin(angle))
            out[k2 + 8 * k1, half] = y.astype(BF16)


def dot(a, b):
    return jnp.dot(a, b, preferred_element_type=F32)


CHUNK = 128
SPECTRUM_ROWS = BLOCKS * ROWS


def filter_spectrum(high_ref, low_ref, dft, out, half):
    def step(i, carry):
        rows = pl.ds(pl.multiple_of(i * CHUNK, CHUNK), CHUNK)
        high, low = high_ref[rows, :], low_ref[rows, :]
        out[half, rows, :] = dot(high, dft[0]) + dot(low, dft[0]) + dot(high, dft[1])
        return carry

    lax.fori_loop(0, SPECTRUM_ROWS // CHUNK, step, 0)


def multiply_spectra(high_ref, low_ref, dft, filters, half, out):
    def step(i, carry):
        rows = pl.ds(pl.multiple_of(i * CHUNK, CHUNK), CHUNK)
        high, low = high_ref[rows, :], low_ref[rows, :]
        g = dot(high, dft[0]) + dot(low, dft[0]) + dot(high, dft[1])
        h = filters[half, rows, :]
        gr, gi, hr, hi = g[:, :LANES], g[:, LANES:], h[:, :LANES], h[:, LANES:]
        product = jnp.concatenate([gr * hr - gi * hi, gr * hi + gi * hr], axis=1)
        high = product.astype(BF16)
        low = (product - high.astype(F32)).astype(BF16)
        out[rows, :] = dot(high, dft[2]) + dot(low, dft[2]) + dot(high, dft[3])
        return carry

    lax.fori_loop(0, SPECTRUM_ROWS // CHUNK, step, 0)


def kernel(
    q_hbm, k_hbm, v_hbm, fw_ref, h_hbm, skip_ref, w_hbm, tw_hbm, dft_hbm,
    out_ref,
    q_in, k_in, v_in, h_in, w_in, twiddle, dft,
    tails, halo, extended, query, gated,
    h_send, g_send, y_send, h_all, g_all, y_all,
    mid, high_ref, low_ref, h_spec, v_spec, mixed, total,
    local_sem, halo_sem, h_sem, g_sem, y_sem, m_sem,
):
    n = lax.axis_size("seq")
    me = lax.axis_index("seq")
    mine = lax.axis_index("ch")
    across = lax.rem(mine + 2, 4)
    beside = mine + 1 - 2 * lax.rem(mine, 2)
    diagonal = lax.rem(beside + 2, 4)

    local = [
        pltpu.make_async_copy(source, target, local_sem.at[i])
        for i, (source, target) in enumerate(
            [(q_hbm, q_in), (k_hbm, k_in), (v_hbm, v_in), (h_hbm, h_in), (tw_hbm, twiddle), (dft_hbm, dft), (w_hbm, w_in)]
        )
    ]
    for copy in local:
        copy.start()

    barrier = pltpu.get_barrier_semaphore()

    def greet(s, carry):
        pl.semaphore_signal(barrier, inc=1, device_id={"seq": lax.rem(me + s, n)}, device_id_type=MESH)
        return carry

    lax.fori_loop(1, n, greet, 0)
    for peer in (across, beside):
        pl.semaphore_signal(barrier, inc=1, device_id={"ch": peer}, device_id_type=MESH)

    for i in range(3):
        local[i].wait()
    for i, x in enumerate((q_in, k_in, v_in)):
        tails[i] = x[112:128, :].astype(F32)[8:16, :]
    local[3].wait()

    def turn(source, target):
        def step(i, carry):
            cols = pl.ds(pl.multiple_of(i * 128, 128), 128)
            block = source[:, cols].T.astype(BF16).reshape(8, ROWS, LANES)
            target[i // 4, pl.ds(lax.rem(i, 4) * 8, 8)] = block
            return carry

        lax.fori_loop(0, 8, step, 0)

    turn(h_in, h_send)

    pl.semaphore_wait(barrier, n - 1 + 2)

    halo_copy = pltpu.make_async_remote_copy(
        src_ref=tails, dst_ref=halo, send_sem=halo_sem.at[0], recv_sem=halo_sem.at[1],
        device_id={"seq": lax.rem(me + 1, n)}, device_id_type=MESH,
    )
    halo_copy.start()

    def scatter(source, target, sems):
        def step(s, carry):
            peer = lax.rem(me + s, n)
            pltpu.make_async_remote_copy(
                src_ref=source.at[:, peer], dst_ref=target.at[me], send_sem=sems.at[0], recv_sem=sems.at[1],
                device_id={"seq": peer}, device_id_type=MESH,
            ).start()
            return carry

        lax.fori_loop(1, n, step, 0)
        target[me] = source[:, me]

    def all_of(ref, sems):
        part = ref.at[pl.ds(0, BLOCKS - 1)]
        return pltpu.make_async_remote_copy(
            src_ref=part, dst_ref=part, send_sem=sems.at[0], recv_sem=sems.at[1],
            device_id={"seq": lax.rem(me + 1, n)}, device_id_type=MESH,
        )

    scatter(h_send, h_all, h_sem)

    halo_copy.wait()
    keep = jnp.where(me == 0, 0.0, 1.0).astype(F32)
    for i, x in enumerate((q_in, k_in, v_in)):
        extended[i, 0:8, :] = halo[i] * keep

        def widen(r, carry):
            rows = pl.multiple_of(r * 16, 16)
            extended[i, pl.ds(rows + 8, 16), :] = x[pl.ds(rows, 16), :].astype(F32)
            return carry

        lax.fori_loop(0, 8, widen, 0)

    def feature(i, cols):
        result = fw_ref[i, 0:1, cols] * extended[i, 8:136, cols]
        result += fw_ref[i, 1:2, cols] * extended[i, 7:135, cols]
        return result + fw_ref[i, 2:3, cols] * extended[i, 6:134, cols]

    def gate(i, carry):
        cols = pl.ds(pl.multiple_of(i * 128, 128), 128)
        value = feature(1, cols) * feature(2, cols)
        gated[:, cols] = value
        g_send[i // 4, pl.ds(lax.rem(i, 4) * 8, 8)] = value.T.astype(BF16).reshape(8, ROWS, LANES)
        return carry

    lax.fori_loop(0, 8, gate, 0)
    scatter(g_send, g_all, g_sem)

    def queries(i, carry):
        cols = pl.ds(pl.multiple_of(i * 128, 128), 128)
        query[:, cols] = feature(0, cols)
        gated[:, cols] = gated[:, cols] * skip_ref[0:1, cols]
        return carry

    lax.fori_loop(0, 8, queries, 0)

    local[4].wait()
    local[5].wait()
    all_of(h_all, h_sem).wait_recv()

    def filters(half, carry):
        forward_blocks(h_all, half, mid, high_ref, low_ref, twiddle)
        filter_spectrum(high_ref, low_ref, dft, h_spec, half)
        return carry

    lax.fori_loop(0, 2, filters, 0)
    all_of(g_all, g_sem).wait_recv()

    def convolve(half, carry):
        forward_blocks(g_all, half, mid, high_ref, low_ref, twiddle)
        multiply_spectra(high_ref, low_ref, dft, h_spec, half, v_spec)
        inverse_blocks(v_spec, mid, y_send, half, twiddle)

        def step(s, inner):
            peer = lax.rem(me + s, n)
            pltpu.make_async_remote_copy(
                src_ref=y_send.at[peer, half], dst_ref=y_all.at[half, me],
                send_sem=y_sem.at[0, half], recv_sem=y_sem.at[1, half],
                device_id={"seq": peer}, device_id_type=MESH,
            ).start()
            return inner

        lax.fori_loop(1, n, step, 0)
        y_all[half, me] = y_send[me, half]
        return carry

    lax.fori_loop(0, 2, convolve, 0)

    def y_done(half):
        part = y_all.at[half, pl.ds(0, BLOCKS - 1)]
        return pltpu.make_async_remote_copy(
            src_ref=part, dst_ref=part, send_sem=y_sem.at[0, half], recv_sem=y_sem.at[1, half],
            device_id={"seq": lax.rem(me + 1, n)}, device_id_type=MESH,
        )

    def share(slot, half, peer, index):
        return pltpu.make_async_remote_copy(
            src_ref=mixed.at[slot, half], dst_ref=mixed.at[slot, half],
            send_sem=m_sem.at[0, index, half], recv_sem=m_sem.at[1, index, half],
            device_id={"ch": peer}, device_id_type=MESH,
        )

    def project(slot, half, first=False):
        rows = pl.ds(pl.multiple_of(slot * 1024 + half * 512, 512), 512)

        def step(j, carry):
            cols = pl.ds(pl.multiple_of(j * 256, 256), 256)
            value = dot(mixed[slot, half], w_in[rows, cols])
            total[:, cols] = value if first else total[:, cols] + value
            return carry

        lax.fori_loop(0, 4, step, 0)

    for half in range(2):
        y_done(half).wait_recv()

        def mix(i, carry):
            cols = pl.ds(pl.multiple_of(half * 512 + i * 128, 128), 128)
            y = y_all[half, pl.ds(i * 8, 8)].astype(F32).reshape(128, LANES).T
            mixed[mine, half, :, pl.ds(pl.multiple_of(i * 128, 128), 128)] = (
                query[:, cols] * (y + gated[:, cols])
            ).astype(BF16)
            return carry

        lax.fori_loop(0, 4, mix, 0)
        share(mine, half, across, 0).start()
        share(mine, half, beside, 1).start()
    local[6].wait()
    for half in range(2):
        project(mine, half, first=half == 0)
        share(across, half, across, 0).wait_recv()
        share(across, half, beside, 2).start()
        project(across, half)
    for half in range(2):
        share(beside, half, beside, 1).wait_recv()
        project(beside, half)
    for half in range(2):
        share(diagonal, half, beside, 2).wait_recv()
        project(diagonal, half)

    def finish(j, carry):
        cols = pl.ds(pl.multiple_of(j * 256, 256), 256)
        out_ref[:, cols] = total[:, cols].astype(BF16)
        return carry

    lax.fori_loop(0, 4, finish, 0)

    all_of(h_all, h_sem).wait_send()
    all_of(g_all, g_sem).wait_send()
    for half in range(2):
        y_done(half).wait_send()
        share(mine, half, across, 0).wait_send()
        share(mine, half, beside, 1).wait_send()
        share(across, half, beside, 2).wait_send()


def shards(query_proj, key_proj, value_proj, feat_weight, long_filter, skip_gain, out_weight):
    twiddle, dft = tables()
    anywhere = pl.BlockSpec(memory_space=pl.ANY)
    vmem = pl.BlockSpec(memory_space=pltpu.VMEM)
    tokens, channels = query_proj.shape
    spectrum = (SPECTRUM_ROWS, 2 * LANES)
    exchanged = (BLOCKS, 2, ROWS, LANES)
    turned = (2, BLOCKS, ROWS, LANES)
    return pl.pallas_call(
        kernel,
        out_shape=jax.ShapeDtypeStruct((tokens, channels), BF16),
        in_specs=[anywhere, anywhere, anywhere, vmem, anywhere, vmem, anywhere, anywhere, anywhere],
        out_specs=vmem,
        scratch_shapes=[
            pltpu.VMEM((tokens, channels), BF16),
            pltpu.VMEM((tokens, channels), BF16),
            pltpu.VMEM((tokens, channels), BF16),
            pltpu.VMEM((tokens, channels), F32),
            pltpu.VMEM(out_weight.shape, BF16),
            pltpu.VMEM(twiddle.shape, F32),
            pltpu.VMEM(dft.shape, BF16),
            pltpu.VMEM((3, 8, channels), F32),
            pltpu.VMEM((3, 8, channels), F32),
            pltpu.VMEM((3, tokens + 8, channels), F32),
            pltpu.VMEM((tokens, channels), F32),
            pltpu.VMEM((tokens, channels), F32),
            pltpu.VMEM(turned, BF16),
            pltpu.VMEM(turned, BF16),
            pltpu.VMEM(exchanged, BF16),
            pltpu.VMEM(exchanged, BF16),
            pltpu.VMEM(exchanged, BF16),
            pltpu.VMEM(turned, BF16),
            pltpu.VMEM((2, 4, 8, ROWS, LANES), F32),
            pltpu.VMEM(spectrum, BF16),
            pltpu.VMEM(spectrum, BF16),
            pltpu.VMEM((2,) + spectrum, F32),
            pltpu.VMEM(spectrum, F32),
            pltpu.VMEM((4, 2, tokens, channels // 2), BF16),
            pltpu.VMEM((tokens, channels), F32),
            pltpu.SemaphoreType.DMA((7,)),
            pltpu.SemaphoreType.DMA((2,)),
            pltpu.SemaphoreType.DMA((2,)),
            pltpu.SemaphoreType.DMA((2,)),
            pltpu.SemaphoreType.DMA((2, 2)),
            pltpu.SemaphoreType.DMA((2, 3, 2)),
        ],
        compiler_params=pltpu.CompilerParams(
            collective_id=0, has_side_effects=True, vmem_limit_bytes=56 * 1024 * 1024
        ),
        name="mixer",
    )(
        query_proj, key_proj, value_proj, feat_weight, long_filter, skip_gain[None, :], out_weight, twiddle, dft,
    )


def solution(mesh):
    placed = (
        P("seq", "ch"),
        P("seq", "ch"),
        P("seq", "ch"),
        P(None, None, "ch"),
        P("seq", "ch"),
        P("ch"),
        P(None, "ch"),
    )
    return jax.shard_map(shards, mesh=mesh, in_specs=placed, out_specs=P("seq", "ch"), check_vma=False)
```

time: 698 us -> 46.4 us (0.07); the launches traced: 690 us -> 45.5 us
  waiting for transfers between devices: 519 us -> 0 us
  starting transfers between devices: 71 us -> 0 us
  other arithmetic: 55.9 us -> 0 us
  Pallas kernels: 0 us -> 43.8 us
  matrix products: 21.2 us -> 0 us
  between operations: 15.7 us -> 0.01 us
    ppermute x16 -> x0, waiting for transfers between devices: 492 us -> none  [the longest x15 492 us: swapped(): return lax.ppermute(value, axis, pairs)]
    ppermute x16 -> x0, starting transfers between devices: 71 us -> none  [the longest x15 67.5 us: swapped(): return lax.ppermute(value, axis, pairs)]
    pallas_call x0 -> x1, Pallas kernels: none -> 43.8 us  [shards(): pl.pallas_call(kernel, out_shape=jax.ShapeDtypeStruct((tokens, channels),...]
    all_gather x1 -> x0, waiting for transfers between devices: 26.8 us -> none  [shards(): lax.all_gather(mixed, 'ch', axis=1, tiled=True)]
    dot_general x13 -> x0, matrix products: 21.2 us -> none  [the longest x12 15.5 us: product_with(): return jnp.einsum('kj,ejc->ekc', matrix, values, precision=exact_mode)]
    another operation x17 -> x0, other arithmetic: 17.7 us -> none  [the longest x8 11.1 us: pair_forward(): updated.append(jnp.stack([real_part, imag_part]))]
    add x13 -> x0, other arithmetic: 17.3 us -> none  [the longest x10 17 us: pair_forward(): combined = peer_part + sign_factor * own_part]
    select_n x5 -> x0, other arithmetic: 7.86 us -> none  [pair_inverse(): upper_part = jnp.where(upper_bit == 1, spectrum, partner)]
  transfers between devices with their start and end apart: 17 -> 0, of which waited for: 15 -> 0; matrix products, arithmetic and copies ran while one was open for 6% -> 0% of each run, Pallas kernels for 0% -> 0%
where the time goes in v1:
time: 46.4 us; the launch traced here: 45.5 us
  Pallas kernels  43.8 us (94%)
  local copies, waits for them, and re-layouts  1.67 us (4%)
    pallas_call x1, Pallas kernels, shards(): pl.pallas_call(kernel, out_shape=jax.ShapeDtypeStruct((tokens, channels),...  43.8 us
    unnamed x1, local copies, waits for them, and re-layouts  1.67 us

profile of v1, /device:TPU:1, one launch (start us, length us, event | category | flops | bytes accessed | tf_op | source)
XLA Modules:
  0.0 45.5 jit_solution(3043176201853625692)
XLA Ops:
  0.0 43.8 %mixer.1 = bf16[128,1024]{1,0:T(8,128)(2,1)} custom-call(bf16[128,1024]{1,0:T(8,128)(2,1)} %q_hbm.1, bf16[128,1024]{1,0:T(8,128)(2,1)} %k_hbm.1, bf16[128,1024]{1,0:T(8,128)(2,1)} %v_hbm.1, f32[3,3,1024]{2,1,0:T(4,128)} %fw_ref.1, f32[128,1024]{1,0:T(8,128)} %h_hbm.1, f32[1,1024]{1,0:T(1,128)} %bitcast.1, bf16[4096,1024]{1,0:T(8,128)(2,1)} %w_hbm.1, ...), custom_call_target="tpu_custom_call" | custom-call | tf_op jit(solution)/shard_map/mixer/pallas_call | solution.py:391
  43.9 1.7 %copy.11 = bf16[128,1024]{1,0:T(8,128)(2,1)} copy(bf16[128,1024]{1,0:T(8,128)(2,1)} %mixer.1) | data formatting | bytes 524288

commit v2 on v1

--- a/solution.py
+++ b/solution.py
@@ -14,6 +14,10 @@
 BLOCKS = 32
 LANES = 128
 ROWS = 16
+FAR_FIRST = sorted(
+    ((dx, dy, dz) for dx in range(4) for dy in range(2) for dz in range(4) if dx + dy + dz),
+    key=lambda d: -(min(d[0], 4 - d[0]) + d[1] + min(d[2], 4 - d[2])),
+)
 HALF_ROOT = float(np.sqrt(0.5))
 
 
@@ -78,7 +82,7 @@
 
 def forward_blocks(source, half, mid, high_ref, low_ref, twiddle):
     for k2 in range(8):
-        x = [source[k2 + 8 * k1, half].astype(F32) for k1 in range(4)]
+        x = [source[half, k2 + 8 * k1].astype(F32) for k1 in range(4)]
         x0, x1, x2, x3 = x
 
         def real_times(value, angle):
@@ -127,7 +131,7 @@
             angle = 2 * np.pi * k1 / 16
             re, im = u[k1]
             y = re if k1 == 0 else re * float(np.cos(angle)) - im * float(np.sin(angle))
-            out[k2 + 8 * k1, half] = y.astype(BF16)
+            out[half, k2 + 8 * k1] = y.astype(BF16)
 
 
 def dot(a, b):
@@ -224,26 +228,29 @@
     )
     halo_copy.start()
 
-    def scatter(source, target, sems):
-        def step(s, carry):
-            peer = lax.rem(me + s, n)
+    xs = [lax.rem(me // 8 + d, 4) * 8 for d in range(4)]
+    ys = [lax.rem(me // 4 + d, 2) * 4 for d in range(2)]
+    zs = [lax.rem(me + d, 4) for d in range(4)]
+
+    def scatter(source, target, half, sems):
+        for dx, dy, dz in FAR_FIRST:
+            peer = xs[dx] + ys[dy] + zs[dz]
             pltpu.make_async_remote_copy(
-                src_ref=source.at[:, peer], dst_ref=target.at[me], send_sem=sems.at[0], recv_sem=sems.at[1],
+                src_ref=source.at[half, peer], dst_ref=target.at[half, me],
+                send_sem=sems.at[0, half], recv_sem=sems.at[1, half],
                 device_id={"seq": peer}, device_id_type=MESH,
             ).start()
-            return carry
-
-        lax.fori_loop(1, n, step, 0)
-        target[me] = source[:, me]
-
-    def all_of(ref, sems):
-        part = ref.at[pl.ds(0, BLOCKS - 1)]
+        target[half, me] = source[half, me]
+
+    def all_of(ref, half, sems):
+        part = ref.at[half, pl.ds(0, BLOCKS - 1)]
         return pltpu.make_async_remote_copy(
-            src_ref=part, dst_ref=part, send_sem=sems.at[0], recv_sem=sems.at[1],
+            src_ref=part, dst_ref=part, send_sem=sems.at[0, half], recv_sem=sems.at[1, half],
             device_id={"seq": lax.rem(me + 1, n)}, device_id_type=MESH,
         )
 
-    scatter(h_send, h_all, h_sem)
+    scatter(h_send, h_all, 0, h_sem)
+    scatter(h_send, h_all, 1, h_sem)
 
     halo_copy.wait()
     keep = jnp.where(me == 0, 0.0, 1.0).astype(F32)
@@ -269,8 +276,9 @@
         g_send[i // 4, pl.ds(lax.rem(i, 4) * 8, 8)] = value.T.astype(BF16).reshape(8, ROWS, LANES)
         return carry
 
-    lax.fori_loop(0, 8, gate, 0)
-    scatter(g_send, g_all, g_sem)
+    for half in range(2):
+        lax.fori_loop(4 * half, 4 * half + 4, gate, 0)
+        scatter(g_send, g_all, half, g_sem)
 
     def queries(i, carry):
         cols = pl.ds(pl.multiple_of(i * 128, 128), 128)
@@ -282,42 +290,24 @@
 
     local[4].wait()
     local[5].wait()
-    all_of(h_all, h_sem).wait_recv()
 
     def filters(half, carry):
+        all_of(h_all, half, h_sem).wait_recv()
         forward_blocks(h_all, half, mid, high_ref, low_ref, twiddle)
         filter_spectrum(high_ref, low_ref, dft, h_spec, half)
         return carry
 
     lax.fori_loop(0, 2, filters, 0)
-    all_of(g_all, g_sem).wait_recv()
 
     def convolve(half, carry):
+        all_of(g_all, half, g_sem).wait_recv()
         forward_blocks(g_all, half, mid, high_ref, low_ref, twiddle)
         multiply_spectra(high_ref, low_ref, dft, h_spec, half, v_spec)
         inverse_blocks(v_spec, mid, y_send, half, twiddle)
-
-        def step(s, inner):
-            peer = lax.rem(me + s, n)
-            pltpu.make_async_remote_copy(
-                src_ref=y_send.at[peer, half], dst_ref=y_all.at[half, me],
-                send_sem=y_sem.at[0, half], recv_sem=y_sem.at[1, half],
-                device_id={"seq": peer}, device_id_type=MESH,
-            ).start()
-            return inner
-
-        lax.fori_loop(1, n, step, 0)
-        y_all[half, me] = y_send[me, half]
+        scatter(y_send, y_all, half, y_sem)
         return carry
 
     lax.fori_loop(0, 2, convolve, 0)
-
-    def y_done(half):
-        part = y_all.at[half, pl.ds(0, BLOCKS - 1)]
-        return pltpu.make_async_remote_copy(
-            src_ref=part, dst_ref=part, send_sem=y_sem.at[0, half], recv_sem=y_sem.at[1, half],
-            device_id={"seq": lax.rem(me + 1, n)}, device_id_type=MESH,
-        )
 
     def share(slot, half, peer, index):
         return pltpu.make_async_remote_copy(
@@ -338,7 +328,7 @@
         lax.fori_loop(0, 4, step, 0)
 
     for half in range(2):
-        y_done(half).wait_recv()
+        all_of(y_all, half, y_sem).wait_recv()
 
         def mix(i, carry):
             cols = pl.ds(pl.multiple_of(half * 512 + i * 128, 128), 128)
@@ -371,10 +361,10 @@
 
     lax.fori_loop(0, 4, finish, 0)
 
-    all_of(h_all, h_sem).wait_send()
-    all_of(g_all, g_sem).wait_send()
-    for half in range(2):
-        y_done(half).wait_send()
+    for half in range(2):
+        all_of(h_all, half, h_sem).wait_send()
+        all_of(g_all, half, g_sem).wait_send()
+        all_of(y_all, half, y_sem).wait_send()
         share(mine, half, across, 0).wait_send()
         share(mine, half, beside, 1).wait_send()
         share(across, half, beside, 2).wait_send()
@@ -386,7 +376,6 @@
     vmem = pl.BlockSpec(memory_space=pltpu.VMEM)
     tokens, channels = query_proj.shape
     spectrum = (SPECTRUM_ROWS, 2 * LANES)
-    exchanged = (BLOCKS, 2, ROWS, LANES)
     turned = (2, BLOCKS, ROWS, LANES)
     return pl.pallas_call(
         kernel,
@@ -408,9 +397,9 @@
             pltpu.VMEM((tokens, channels), F32),
             pltpu.VMEM(turned, BF16),
             pltpu.VMEM(turned, BF16),
-            pltpu.VMEM(exchanged, BF16),
-            pltpu.VMEM(exchanged, BF16),
-            pltpu.VMEM(exchanged, BF16),
+            pltpu.VMEM(turned, BF16),
+            pltpu.VMEM(turned, BF16),
+            pltpu.VMEM(turned, BF16),
             pltpu.VMEM(turned, BF16),
             pltpu.VMEM((2, 4, 8, ROWS, LANES), F32),
             pltpu.VMEM(spectrum, BF16),
@@ -421,8 +410,8 @@
             pltpu.VMEM((tokens, channels), F32),
             pltpu.SemaphoreType.DMA((7,)),
             pltpu.SemaphoreType.DMA((2,)),
-            pltpu.SemaphoreType.DMA((2,)),
-            pltpu.SemaphoreType.DMA((2,)),
+            pltpu.SemaphoreType.DMA((2, 2)),
+            pltpu.SemaphoreType.DMA((2, 2)),
             pltpu.SemaphoreType.DMA((2, 2)),
             pltpu.SemaphoreType.DMA((2, 3, 2)),
         ],

time: 46.4 us -> 43.8 us (0.944)
  the two profiles are of different devices: /device:TPU:1 before, /device:TPU:0 now
where the time goes in v2:
time: 43.8 us; the launch traced here: 43.6 us
  Pallas kernels  41.9 us (96%)
  local copies, waits for them, and re-layouts  1.67 us (4%)
    pallas_call x1, Pallas kernels, shards(): pl.pallas_call(kernel, out_shape=jax.ShapeDtypeStruct((tokens, channels),...  41.9 us
    unnamed x1, local copies, waits for them, and re-layouts  1.67 us

profile of v2, /device:TPU:0, one launch (start us, length us, event | category | flops | bytes accessed | tf_op | source)
XLA Modules:
  0.0 43.6 jit_solution(7913210662018965360)
XLA Ops:
  0.0 41.9 %mixer.1 = bf16[128,1024]{1,0:T(8,128)(2,1)} custom-call(bf16[128,1024]{1,0:T(8,128)(2,1)} %q_hbm.1, bf16[128,1024]{1,0:T(8,128)(2,1)} %k_hbm.1, bf16[128,1024]{1,0:T(8,128)(2,1)} %v_hbm.1, f32[3,3,1024]{2,1,0:T(4,128)} %fw_ref.1, f32[128,1024]{1,0:T(8,128)} %h_hbm.1, f32[1,1024]{1,0:T(1,128)} %bitcast.1, bf16[4096,1024]{1,0:T(8,128)(2,1)} %w_hbm.1, ...), custom_call_target="tpu_custom_call" | custom-call | tf_op jit(solution)/shard_map/mixer/pallas_call | solution.py:380
  42.0 1.7 %copy.11 = bf16[128,1024]{1,0:T(8,128)(2,1)} copy(bf16[128,1024]{1,0:T(8,128)(2,1)} %mixer.1) | data formatting | bytes 524288

commit v3 on v2

v3 whole, which is shorter than its diff:
```python
import functools

import jax
import jax.numpy as jnp
import numpy as np
from jax import lax
from jax.experimental import pallas as pl
from jax.experimental.pallas import tpu as pltpu
from jax.sharding import PartitionSpec as P

F32 = jnp.float32
BF16 = jnp.bfloat16
MESH = pl.DeviceIdType.MESH
BLOCKS = 32
LANES = 128
PARTS = 2
ROWS = 32 // PARTS
WIDTH = BLOCKS * ROWS
TILES = 128 // ROWS
FAR_FIRST = sorted(
    ((dx, dy, dz) for dx in range(4) for dy in range(2) for dz in range(4) if dx + dy + dz),
    key=lambda d: -(min(d[0], 4 - d[0]) + d[1] + min(d[2], 4 - d[2])),
)
HALF_ROOT = float(np.sqrt(0.5))


def tables():
    lane = np.arange(LANES)
    theta = 2 * np.pi * (np.arange(BLOCKS)[:, None] + 0.25) * lane[None, :] / (BLOCKS * LANES)
    twiddle = np.stack([np.cos(theta), np.sin(theta)]).astype(np.float32)
    phase = 2 * np.pi * (lane[:, None] * lane[None, :] % LANES) / LANES
    c, s = np.cos(phase), np.sin(phase)
    forward = np.block([[c, -s], [s, c]])
    inverse = np.block([[c, s], [-s, c]]) / (BLOCKS * LANES)
    parts = []
    for matrix in (forward, inverse):
        high = matrix.astype(BF16)
        parts += [high, (matrix - high.astype(np.float64)).astype(BF16)]
    return jnp.asarray(twiddle), jnp.asarray(np.stack(parts))


def times(value, angle):
    re, im = value
    c, s = float(np.cos(angle)), float(np.sin(angle))
    if abs(angle) < 1e-12:
        return re, im
    return re * c - im * s, im * c + re * s


def fft4(x, sign):
    (ar, ai), (br, bi), (cr, ci), (dr, di) = x
    er, ei, fr, fi = ar + cr, ai + ci, ar - cr, ai - ci
    gr, gi, hr, hi = br + dr, bi + di, br - dr, bi - di
    if sign < 0:
        jr, ji = hi, -hr
    else:
        jr, ji = -hi, hr
    return [(er + gr, ei + gi), (fr + jr, fi + ji), (er - gr, ei - gi), (fr - jr, fi - ji)]


def fft8(x, sign):
    even = fft4(x[0::2], sign)
    odd = fft4(x[1::2], sign)
    o1r, o1i = odd[1]
    o2r, o2i = odd[2]
    o3r, o3i = odd[3]
    if sign < 0:
        odd[1] = ((o1r + o1i) * HALF_ROOT, (o1i - o1r) * HALF_ROOT)
        odd[2] = (o2i, -o2r)
        odd[3] = ((o3i - o3r) * HALF_ROOT, (-o3i - o3r) * HALF_ROOT)
    else:
        odd[1] = ((o1r - o1i) * HALF_ROOT, (o1i + o1r) * HALF_ROOT)
        odd[2] = (-o2i, o2r)
        odd[3] = ((-o3r - o3i) * HALF_ROOT, (o3r - o3i) * HALF_ROOT)
    low = [(e[0] + o[0], e[1] + o[1]) for e, o in zip(even, odd)]
    high = [(e[0] - o[0], e[1] - o[1]) for e, o in zip(even, odd)]
    return low + high


def store_split(high_ref, low_ref, index, value):
    high = value.astype(BF16)
    high_ref[index] = high
    low_ref[index] = (value - high.astype(F32)).astype(BF16)


def forward_blocks(source, half, mid, high_ref, low_ref, twiddle):
    for k2 in range(8):
        x = [source[half, k2 + 8 * k1].astype(F32) for k1 in range(4)]
        x0, x1, x2, x3 = x

        def real_times(value, angle):
            return value * float(np.cos(angle)), value * float(np.sin(angle))

        t1 = real_times(x1, -2 * np.pi / 16)
        t2 = real_times(x2, -2 * np.pi * 2 / 16)
        t3 = real_times(x3, -2 * np.pi * 3 / 16)
        er, ei, fr, fi = x0 + t2[0], t2[1], x0 - t2[0], -t2[1]
        gr, gi, hr, hi = t1[0] + t3[0], t1[1] + t3[1], t1[0] - t3[0], t1[1] - t3[1]
        results = [(er + gr, ei + gi), (fr + hi, fi - hr), (er - gr, ei - gi), (fr - hi, fi + hr)]
        for f1 in range(4):
            re, im = times(results[f1], -2 * np.pi * k2 * (0.25 + f1) / 32)
            mid[0, f1, k2] = re
            mid[1, f1, k2] = im
    for f1 in range(4):
        spectrum = fft8([(mid[0, f1, k2], mid[1, f1, k2]) for k2 in range(8)], -1)
        for f2 in range(8):
            f = f1 + 4 * f2
            c = twiddle[0, f : f + 1, :]
            s = twiddle[1, f : f + 1, :]
            re, im = spectrum[f2]
            rows = pl.ds(f * ROWS, ROWS)
            store_split(high_ref, low_ref, (rows, pl.ds(0, LANES)), re * c + im * s)
            store_split(high_ref, low_ref, (rows, pl.ds(LANES, LANES)), im * c - re * s)


def inverse_blocks(source, mid, out, half, twiddle, feature_q, skipped):
    for f1 in range(4):
        values = []
        for f2 in range(8):
            f = f1 + 4 * f2
            c = twiddle[0, f : f + 1, :]
            s = twiddle[1, f : f + 1, :]
            re = source[pl.ds(f * ROWS, ROWS), pl.ds(0, LANES)]
            im = source[pl.ds(f * ROWS, ROWS), pl.ds(LANES, LANES)]
            values.append((re * c - im * s, im * c + re * s))
        spectrum = fft8(values, 1)
        for k2 in range(8):
            re, im = times(spectrum[k2], 2 * np.pi * k2 * (0.25 + f1) / 32)
            mid[0, f1, k2] = re
            mid[1, f1, k2] = im
    for k2 in range(8):
        u = fft4([(mid[0, f1, k2], mid[1, f1, k2]) for f1 in range(4)], 1)
        for k1 in range(4):
            angle = 2 * np.pi * k1 / 16
            re, im = u[k1]
            y = re if k1 == 0 else re * float(np.cos(angle)) - im * float(np.sin(angle))
            k = k2 + 8 * k1
            out[half, k] = (feature_q[k] * (y + skipped[k])).astype(BF16)


def dot(a, b):
    return jnp.dot(a, b, preferred_element_type=F32)


CHUNK = 128
SPECTRUM_ROWS = BLOCKS * ROWS


def filter_spectrum(high_ref, low_ref, dft, out, half):
    def step(i, carry):
        rows = pl.ds(pl.multiple_of(i * CHUNK, CHUNK), CHUNK)
        high, low = high_ref[rows, :], low_ref[rows, :]
        out[half, rows, :] = dot(high, dft[0]) + dot(low, dft[0]) + dot(high, dft[1])
        return carry

    lax.fori_loop(0, SPECTRUM_ROWS // CHUNK, step, 0)


def multiply_spectra(high_ref, low_ref, dft, filters, half, out):
    def step(i, carry):
        rows = pl.ds(pl.multiple_of(i * CHUNK, CHUNK), CHUNK)
        high, low = high_ref[rows, :], low_ref[rows, :]
        g = dot(high, dft[0]) + dot(low, dft[0]) + dot(high, dft[1])
        h = filters[half, rows, :]
        gr, gi, hr, hi = g[:, :LANES], g[:, LANES:], h[:, :LANES], h[:, LANES:]
        product = jnp.concatenate([gr * hr - gi * hi, gr * hi + gi * hr], axis=1)
        high = product.astype(BF16)
        low = (product - high.astype(F32)).astype(BF16)
        out[rows, :] = dot(high, dft[2]) + dot(low, dft[2]) + dot(high, dft[3])
        return carry

    lax.fori_loop(0, SPECTRUM_ROWS // CHUNK, step, 0)


def kernel(
    q_hbm, k_hbm, v_hbm, fw_hbm, h_hbm, skip_hbm, w_hbm, tw_hbm, dft_hbm,
    out_ref,
    q_in, k_in, v_in, fw_ref, h_in, skip_ref, w_in, twiddle, dft,
    tails, halo, extended, columns, feature_q, skipped,
    h_send, g_send, q_send, m_send, h_all, g_all, q_all,
    mid, high_ref, low_ref, h_spec, v_spec, mixed, total, out_stage,
    local_sem, halo_sem, h_sem, g_sem, q_sem, m_sem, swap_sem, out_sem,
):
    n = lax.axis_size("seq")
    me = lax.axis_index("seq")
    mine = lax.axis_index("ch")
    across = lax.rem(mine + 2, 4)
    beside = mine + 1 - 2 * lax.rem(mine, 2)
    diagonal = lax.rem(beside + 2, 4)

    xs = [lax.rem(me // 8 + d, 4) * 8 for d in range(4)]
    ys = [lax.rem(me // 4 + d, 2) * 4 for d in range(2)]
    zs = [lax.rem(me + d, 4) for d in range(4)]
    peers = [xs[dx] + ys[dy] + zs[dz] for dx, dy, dz in FAR_FIRST]

    barrier = pltpu.get_barrier_semaphore()
    for peer in peers:
        pl.semaphore_signal(barrier, inc=1, device_id={"seq": peer}, device_id_type=MESH)
    for target in (across, beside):
        pl.semaphore_signal(barrier, inc=1, device_id={"ch": target}, device_id_type=MESH)

    pairs = [
        (k_hbm, k_in), (v_hbm, v_in), (q_hbm, q_in), (h_hbm, h_in), (fw_hbm, fw_ref), (skip_hbm, skip_ref),
        (tw_hbm, twiddle), (dft_hbm, dft), (w_hbm, w_in),
    ]
    local = [pltpu.make_async_copy(source, target, local_sem.at[i]) for i, (source, target) in enumerate(pairs)]
    for copy in local:
        copy.start()

    for i in range(3):
        local[i].wait()
    ends = [x[112:128, :].astype(F32)[14:16, :] for x in (k_in, v_in)]
    tails[...] = jnp.concatenate(ends * 2, axis=0)
    for i in range(3, 6):
        local[i].wait()

    def turned(block):
        return block.T.astype(BF16).reshape(TILES, ROWS, LANES)

    def place(i):
        return i * 128 // WIDTH, pl.ds(lax.rem(i * 128, WIDTH) // ROWS, TILES)

    def turn(i, carry):
        cols = pl.ds(pl.multiple_of(i * 128, 128), 128)
        part, blocks = place(i)
        h_send[part, blocks] = turned(h_in[:, cols])
        q_send[part, blocks] = turned(q_in[:, cols].astype(F32))
        rows = jnp.concatenate([skip_ref[0:1, cols], fw_ref[0, :, cols], jnp.zeros((124, 128), F32)], axis=0)
        columns[cols, :] = rows.T
        return carry

    lax.fori_loop(0, 8, turn, 0)

    pl.semaphore_wait(barrier, n - 1 + 2)

    halo_copy = pltpu.make_async_remote_copy(
        src_ref=tails, dst_ref=halo, send_sem=halo_sem.at[0], recv_sem=halo_sem.at[1],
        device_id={"seq": lax.rem(me + 1, n)}, device_id_type=MESH,
    )
    halo_copy.start()

    def scatter(source, target, part, sems):
        for peer in peers:
            pltpu.make_async_remote_copy(
                src_ref=source.at[part, peer], dst_ref=target.at[part, me],
                send_sem=sems.at[0, part], recv_sem=sems.at[1, part],
                device_id={"seq": peer}, device_id_type=MESH,
            ).start()
        target[part, me] = source[part, me]

    def all_of(ref, part, sems):
        view = ref.at[part, pl.ds(0, BLOCKS - 1)]
        return pltpu.make_async_remote_copy(
            src_ref=view, dst_ref=view, send_sem=sems.at[0, part], recv_sem=sems.at[1, part],
            device_id={"seq": lax.rem(me + 1, n)}, device_id_type=MESH,
        )

    def scatter_filters(part, carry):
        scatter(h_send, h_all, part, h_sem)
        return carry

    lax.fori_loop(0, PARTS, scatter_filters, 0)

    halo_copy.wait()
    keep = jnp.where(me == 0, 0.0, 1.0).astype(F32)
    for i, x in enumerate((k_in, v_in)):
        extended[i, 6:8, :] = halo[2 * i : 2 * i + 2, :] * keep

        def widen(r, carry):
            rows = pl.multiple_of(r * 16, 16)
            extended[i, pl.ds(rows + 8, 16), :] = x[pl.ds(rows, 16), :].astype(F32)
            return carry

        lax.fori_loop(0, 8, widen, 0)

    def feature(i, cols):
        result = fw_ref[i + 1, 0:1, cols] * extended[i, 8:136, cols]
        result += fw_ref[i + 1, 1:2, cols] * extended[i, 7:135, cols]
        return result + fw_ref[i + 1, 2:3, cols] * extended[i, 6:134, cols]

    def gate(i, carry):
        cols = pl.ds(pl.multiple_of(i * 128, 128), 128)
        part, blocks = place(i)
        g_send[part, blocks] = turned(feature(0, cols) * feature(1, cols))
        return carry

    def gate_part(part, carry):
        lax.fori_loop(part * (8 // PARTS), (part + 1) * (8 // PARTS), gate, 0)
        scatter(g_send, g_all, part, g_sem)
        scatter(q_send, q_all, part, q_sem)
        return carry

    lax.fori_loop(0, PARTS, gate_part, 0)

    local[6].wait()
    local[7].wait()

    def filters(part, carry):
        all_of(h_all, part, h_sem).wait_recv()
        forward_blocks(h_all, part, mid, high_ref, low_ref, twiddle)
        filter_spectrum(high_ref, low_ref, dft, h_spec, part)
        return carry

    lax.fori_loop(0, PARTS, filters, 0)

    lane = lax.broadcasted_iota(jnp.int32, (ROWS, LANES), 1)

    def query_features(part):
        own = columns[pl.ds(pl.multiple_of(part * WIDTH + me * ROWS, ROWS), ROWS), :]
        gain, w0, w1, w2 = [jnp.broadcast_to(own[:, i : i + 1], (ROWS, LANES)) for i in range(4)]
        before1 = before2 = jnp.zeros((ROWS, LANES), F32)
        for k in range(BLOCKS):
            x = q_all[part, k].astype(F32)
            now1, now2 = pltpu.roll(x, 1, 1), pltpu.roll(x, 2, 1)
            shifted = w1 * jnp.where(lane < 1, before1, now1) + w2 * jnp.where(lane < 2, before2, now2)
            feature_q[k] = w0 * x + shifted
            skipped[k] = gain * g_all[part, k].astype(F32)
            before1, before2 = now1, now2

    def convolve(part, carry):
        all_of(g_all, part, g_sem).wait_recv()
        forward_blocks(g_all, part, mid, high_ref, low_ref, twiddle)
        multiply_spectra(high_ref, low_ref, dft, h_spec, part, v_spec)
        all_of(q_all, part, q_sem).wait_recv()
        query_features(part)
        inverse_blocks(v_spec, mid, m_send, part, twiddle, feature_q, skipped)
        for peer in peers + [me]:
            for side, target in ((1, across), (0, mine)):
                if side == 0 and peer is me:
                    continue
                pltpu.make_async_remote_copy(
                    src_ref=m_send.at[part, peer], dst_ref=mixed.at[mine, part, me],
                    send_sem=m_sem.at[0, side, part], recv_sem=m_sem.at[1, side, part],
                    device_id={"seq": peer, "ch": target}, device_id_type=MESH,
                ).start()
        mixed[mine, part, me] = m_send[part, me]
        return carry

    lax.fori_loop(0, PARTS, convolve, 0)

    def arrived(side, part):
        view = mixed.at[0, part, pl.ds(0, BLOCKS - 1 + side)]
        return pltpu.make_async_remote_copy(
            src_ref=view, dst_ref=view, send_sem=m_sem.at[0, side, part], recv_sem=m_sem.at[1, side, part],
            device_id={"ch": across}, device_id_type=MESH,
        )

    def swap(slot, side, part):
        return pltpu.make_async_remote_copy(
            src_ref=mixed.at[slot, part], dst_ref=mixed.at[slot, part],
            send_sem=swap_sem.at[0, side, part], recv_sem=swap_sem.at[1, side, part],
            device_id={"ch": beside}, device_id_type=MESH,
        )

    def product(tokens, slot, part, cols):
        rows = pl.ds(pl.multiple_of(slot * 1024 + part * WIDTH, WIDTH), WIDTH)
        return dot(tokens, w_in[rows, cols])

    def by_token(slot, part):
        return mixed[slot, part].reshape(WIDTH, LANES).astype(F32).T.astype(BF16)

    def project(slot, part):
        tokens = by_token(slot, part)

        def step(j, carry):
            cols = pl.ds(pl.multiple_of(j * 256, 256), 256)
            total[:, cols] = total[:, cols] + product(tokens, slot, part, cols)
            return carry

        lax.fori_loop(0, 4, step, 0)

    total[...] = jnp.zeros_like(total)
    local[8].wait()
    for part in range(PARTS):
        arrived(0, part).wait_recv()
        swap(mine, 0, part).start()
        project(mine, part)
        arrived(1, part).wait_recv()
        swap(across, 1, part).start()
        project(across, part)
        swap(beside, 0, part).wait_recv()
        project(beside, part)
        swap(diagonal, 1, part).wait_recv()
        if part < PARTS - 1:
            project(diagonal, part)
    tokens = by_token(diagonal, PARTS - 1)

    def finish(j):
        cols = pl.ds(pl.multiple_of(j * 256, 256), 256)
        return pltpu.make_async_copy(out_stage.at[:, cols], out_ref.at[:, cols], out_sem.at[j])

    def last(j, carry):
        cols = pl.ds(pl.multiple_of(j * 256, 256), 256)
        out_stage[:, cols] = (total[:, cols] + product(tokens, diagonal, PARTS - 1, cols)).astype(BF16)
        finish(j).start()
        return carry

    lax.fori_loop(0, 4, last, 0)

    for part in range(PARTS):
        all_of(h_all, part, h_sem).wait_send()
        all_of(g_all, part, g_sem).wait_send()
        all_of(q_all, part, q_sem).wait_send()
        for side in range(2):
            arrived(side, part).wait_send()
            swap(mine, side, part).wait_send()
    for j in range(4):
        finish(j).wait()


def shards(query_proj, key_proj, value_proj, feat_weight, long_filter, skip_gain, out_weight):
    twiddle, dft = tables()
    anywhere = pl.BlockSpec(memory_space=pl.ANY)
    tokens, channels = query_proj.shape
    spectrum = (SPECTRUM_ROWS, 2 * LANES)
    turned = (PARTS, BLOCKS, ROWS, LANES)
    return pl.pallas_call(
        kernel,
        out_shape=jax.ShapeDtypeStruct((tokens, channels), BF16),
        in_specs=[anywhere] * 9,
        out_specs=anywhere,
        scratch_shapes=[
            pltpu.VMEM((tokens, channels), BF16),
            pltpu.VMEM((tokens, channels), BF16),
            pltpu.VMEM((tokens, channels), BF16),
            pltpu.VMEM(feat_weight.shape, F32),
            pltpu.VMEM((tokens, channels), F32),
            pltpu.VMEM((1, channels), F32),
            pltpu.VMEM(out_weight.shape, BF16),
            pltpu.VMEM(twiddle.shape, F32),
            pltpu.VMEM(dft.shape, BF16),
            pltpu.VMEM((8, channels), F32),
            pltpu.VMEM((8, channels), F32),
            pltpu.VMEM((2, tokens + 8, channels), F32),
            pltpu.VMEM((channels, LANES), F32),
            pltpu.VMEM((BLOCKS, ROWS, LANES), F32),
            pltpu.VMEM((BLOCKS, ROWS, LANES), F32),
            pltpu.VMEM(turned, BF16),
            pltpu.VMEM(turned, BF16),
            pltpu.VMEM(turned, BF16),
            pltpu.VMEM(turned, BF16),
            pltpu.VMEM(turned, BF16),
            pltpu.VMEM(turned, BF16),
            pltpu.VMEM(turned, BF16),
            pltpu.VMEM((2, 4, 8, ROWS, LANES), F32),
            pltpu.VMEM(spectrum, BF16),
            pltpu.VMEM(spectrum, BF16),
            pltpu.VMEM((PARTS,) + spectrum, F32),
            pltpu.VMEM(spectrum, F32),
            pltpu.VMEM((4,) + turned, BF16),
            pltpu.VMEM((tokens, channels), F32),
            pltpu.VMEM((tokens, channels), BF16),
            pltpu.SemaphoreType.DMA((9,)),
            pltpu.SemaphoreType.DMA((2,)),
            pltpu.SemaphoreType.DMA((2, PARTS)),
            pltpu.SemaphoreType.DMA((2, PARTS)),
            pltpu.SemaphoreType.DMA((2, PARTS)),
            pltpu.SemaphoreType.DMA((2, 2, PARTS)),
            pltpu.SemaphoreType.DMA((2, 2, PARTS)),
            pltpu.SemaphoreType.DMA((4,)),
        ],
        compiler_params=pltpu.CompilerParams(
            collective_id=0, has_side_effects=True, vmem_limit_bytes=56 * 1024 * 1024
        ),
        name="mixer",
    )(
        query_proj, key_proj, value_proj, feat_weight, long_filter, skip_gain[None, :], out_weight, twiddle, dft,
    )


def solution(mesh):
    placed = (
        P("seq", "ch"),
        P("seq", "ch"),
        P("seq", "ch"),
        P(None, None, "ch"),
        P("seq", "ch"),
        P("ch"),
        P(None, "ch"),
    )
    return jax.shard_map(shards, mesh=mesh, in_specs=placed, out_specs=P("seq", "ch"), check_vma=False)
```

time: 43.8 us -> 38.8 us (0.89)
  the two profiles are of different devices: /device:TPU:0 before, /device:TPU:1 now
where the time goes in v3:
time: 38.8 us; the launch traced here: 38.7 us
  Pallas kernels  37 us (95%)
  local copies, waits for them, and re-layouts  1.67 us (4%)
    pallas_call x1, Pallas kernels, shards(): pl.pallas_call(kernel, out_shape=jax.ShapeDtypeStruct((tokens, channels),...  37 us
    unnamed x1, local copies, waits for them, and re-layouts  1.67 us

profile of v3, /device:TPU:1, one launch (start us, length us, event | category | flops | bytes accessed | tf_op | source)
XLA Modules:
  0.0 38.7 jit_solution(15046846347816593225)
XLA Ops:
  0.0 37.0 %mixer.1 = bf16[128,1024]{1,0:T(8,128)(2,1)} custom-call(bf16[128,1024]{1,0:T(8,128)(2,1)} %q_hbm.1, bf16[128,1024]{1,0:T(8,128)(2,1)} %k_hbm.1, bf16[128,1024]{1,0:T(8,128)(2,1)} %v_hbm.1, f32[3,3,1024]{2,1,0:T(4,128)} %fw_hbm.1, f32[128,1024]{1,0:T(8,128)} %h_hbm.1, f32[1,1024]{1,0:T(1,128)} %bitcast.1, bf16[4096,1024]{1,0:T(8,128)(2,1)} %w_hbm.1, ...), custom_call_target="tpu_custom_call" | custom-call | tf_op jit(solution)/shard_map/mixer/pallas_call | solution.py:417
  37.0 1.7 %copy.11 = bf16[128,1024]{1,0:T(8,128)(2,1)} copy(bf16[128,1024]{1,0:T(8,128)(2,1)} %mixer.1) | data formatting | bytes 524288

commit v4 on v3

--- a/solution.py
+++ b/solution.py
@@ -142,7 +142,7 @@
     return jnp.dot(a, b, preferred_element_type=F32)
 
 
-CHUNK = 128
+CHUNK = 512
 SPECTRUM_ROWS = BLOCKS * ROWS
 
 
@@ -210,12 +210,12 @@
     for i in range(3):
         local[i].wait()
     ends = [x[112:128, :].astype(F32)[14:16, :] for x in (k_in, v_in)]
-    tails[...] = jnp.concatenate(ends * 2, axis=0)
+    tails[...] = jnp.concatenate(ends, axis=0).astype(BF16)
     for i in range(3, 6):
         local[i].wait()
 
     def turned(block):
-        return block.T.astype(BF16).reshape(TILES, ROWS, LANES)
+        return block.astype(BF16).T.reshape(TILES, ROWS, LANES)
 
     def place(i):
         return i * 128 // WIDTH, pl.ds(lax.rem(i * 128, WIDTH) // ROWS, TILES)
@@ -224,12 +224,19 @@
         cols = pl.ds(pl.multiple_of(i * 128, 128), 128)
         part, blocks = place(i)
         h_send[part, blocks] = turned(h_in[:, cols])
-        q_send[part, blocks] = turned(q_in[:, cols].astype(F32))
-        rows = jnp.concatenate([skip_ref[0:1, cols], fw_ref[0, :, cols], jnp.zeros((124, 128), F32)], axis=0)
-        columns[cols, :] = rows.T
+        q_send[part, blocks] = turned(q_in[:, cols])
         return carry
 
     lax.fori_loop(0, 8, turn, 0)
+
+    for i, x in enumerate((k_in, v_in)):
+
+        def widen(r, carry):
+            rows = pl.multiple_of(r * 16, 16)
+            extended[i, pl.ds(rows + 8, 16), :] = x[pl.ds(rows, 16), :].astype(F32)
+            return carry
+
+        lax.fori_loop(0, 8, widen, 0)
 
     pl.semaphore_wait(barrier, n - 1 + 2)
 
@@ -255,23 +262,18 @@
             device_id={"seq": lax.rem(me + 1, n)}, device_id_type=MESH,
         )
 
-    def scatter_filters(part, carry):
-        scatter(h_send, h_all, part, h_sem)
-        return carry
-
-    lax.fori_loop(0, PARTS, scatter_filters, 0)
+    scatter(h_send, h_all, 0, h_sem)
+    scatter(h_send, h_all, 1, h_sem)
+
+    for i in range(8):
+        cols = pl.ds(i * 128, 128)
+        rows = jnp.concatenate([skip_ref[0:1, cols], fw_ref[0, :, cols], jnp.zeros((4, 128), F32)], axis=0)
+        columns[cols, :] = rows.T
 
     halo_copy.wait()
-    keep = jnp.where(me == 0, 0.0, 1.0).astype(F32)
-    for i, x in enumerate((k_in, v_in)):
-        extended[i, 6:8, :] = halo[2 * i : 2 * i + 2, :] * keep
-
-        def widen(r, carry):
-            rows = pl.multiple_of(r * 16, 16)
-            extended[i, pl.ds(rows + 8, 16), :] = x[pl.ds(rows, 16), :].astype(F32)
-            return carry
-
-        lax.fori_loop(0, 8, widen, 0)
+    before = halo[...].astype(F32) * jnp.where(me == 0, 0.0, 1.0).astype(F32)
+    for i in range(2):
+        extended[i, 6:8, :] = before[2 * i : 2 * i + 2, :]
 
     def feature(i, cols):
         result = fw_ref[i + 1, 0:1, cols] * extended[i, 8:136, cols]
@@ -324,10 +326,8 @@
         all_of(q_all, part, q_sem).wait_recv()
         query_features(part)
         inverse_blocks(v_spec, mid, m_send, part, twiddle, feature_q, skipped)
-        for peer in peers + [me]:
-            for side, target in ((1, across), (0, mine)):
-                if side == 0 and peer is me:
-                    continue
+        for side, target in ((1, across), (0, mine)):
+            for peer in peers + [me] * side:
                 pltpu.make_async_remote_copy(
                     src_ref=m_send.at[part, peer], dst_ref=mixed.at[mine, part, me],
                     send_sem=m_sem.at[0, side, part], recv_sem=m_sem.at[1, side, part],
@@ -362,22 +362,19 @@
     def project(slot, part):
         tokens = by_token(slot, part)
 
-        def step(j, carry):
-            cols = pl.ds(pl.multiple_of(j * 256, 256), 256)
+        for j in range(4):
+            cols = pl.ds(j * 256, 256)
             total[:, cols] = total[:, cols] + product(tokens, slot, part, cols)
-            return carry
-
-        lax.fori_loop(0, 4, step, 0)
 
     total[...] = jnp.zeros_like(total)
     local[8].wait()
     for part in range(PARTS):
+        arrived(1, part).wait_recv()
+        swap(across, 1, part).start()
+        project(across, part)
         arrived(0, part).wait_recv()
         swap(mine, 0, part).start()
         project(mine, part)
-        arrived(1, part).wait_recv()
-        swap(across, 1, part).start()
-        project(across, part)
         swap(beside, 0, part).wait_recv()
         project(beside, part)
         swap(diagonal, 1, part).wait_recv()
@@ -386,16 +383,13 @@
     tokens = by_token(diagonal, PARTS - 1)
 
     def finish(j):
-        cols = pl.ds(pl.multiple_of(j * 256, 256), 256)
+        cols = pl.ds(j * 256, 256)
         return pltpu.make_async_copy(out_stage.at[:, cols], out_ref.at[:, cols], out_sem.at[j])
 
-    def last(j, carry):
-        cols = pl.ds(pl.multiple_of(j * 256, 256), 256)
+    for j in range(4):
+        cols = pl.ds(j * 256, 256)
         out_stage[:, cols] = (total[:, cols] + product(tokens, diagonal, PARTS - 1, cols)).astype(BF16)
         finish(j).start()
-        return carry
-
-    lax.fori_loop(0, 4, last, 0)
 
     for part in range(PARTS):
         all_of(h_all, part, h_sem).wait_send()
@@ -429,10 +423,10 @@
             pltpu.VMEM(out_weight.shape, BF16),
             pltpu.VMEM(twiddle.shape, F32),
             pltpu.VMEM(dft.shape, BF16),
-            pltpu.VMEM((8, channels), F32),
-            pltpu.VMEM((8, channels), F32),
+            pltpu.VMEM((4, channels), BF16),
+            pltpu.VMEM((4, channels), BF16),
             pltpu.VMEM((2, tokens + 8, channels), F32),
-            pltpu.VMEM((channels, LANES), F32),
+            pltpu.VMEM((channels, 8), F32),
             pltpu.VMEM((BLOCKS, ROWS, LANES), F32),
             pltpu.VMEM((BLOCKS, ROWS, LANES), F32),
             pltpu.VMEM(turned, BF16),

time: 38.8 us -> 34.2 us (0.88)
  Pallas kernels: 37 us -> 32.4 us
    pallas_call x1, Pallas kernels: 37 us -> 32.4 us  [shards(): pl.pallas_call(kernel, out_shape=jax.ShapeDtypeStruct((tokens, channels),...]
where the time goes in v4:
time: 34.2 us; the launch traced here: 34.1 us
  Pallas kernels  32.4 us (95%)
  local copies, waits for them, and re-layouts  1.67 us (5%)
    pallas_call x1, Pallas kernels, shards(): pl.pallas_call(kernel, out_shape=jax.ShapeDtypeStruct((tokens, channels),...  32.4 us
    unnamed x1, local copies, waits for them, and re-layouts  1.67 us

profile of v4, /device:TPU:1, one launch (start us, length us, event | category | flops | bytes accessed | tf_op | source)
XLA Modules:
  0.0 34.1 jit_solution(15199003945526299405)
XLA Ops:
  0.0 32.4 %mixer.1 = bf16[128,1024]{1,0:T(8,128)(2,1)} custom-call(bf16[128,1024]{1,0:T(8,128)(2,1)} %q_hbm.1, bf16[128,1024]{1,0:T(8,128)(2,1)} %k_hbm.1, bf16[128,1024]{1,0:T(8,128)(2,1)} %v_hbm.1, f32[3,3,1024]{2,1,0:T(4,128)} %fw_hbm.1, f32[128,1024]{1,0:T(8,128)} %h_hbm.1, f32[1,1024]{1,0:T(1,128)} %bitcast.1, bf16[4096,1024]{1,0:T(8,128)(2,1)} %w_hbm.1, ...), custom_call_target="tpu_custom_call" | custom-call | tf_op jit(solution)/shard_map/mixer/pallas_call | solution.py:411
  32.4 1.7 %copy.11 = bf16[128,1024]{1,0:T(8,128)(2,1)} copy(bf16[128,1024]{1,0:T(8,128)(2,1)} %mixer.1) | data formatting | bytes 524288

commit v5 on v4

--- a/solution.py
+++ b/solution.py
@@ -113,7 +113,7 @@
             store_split(high_ref, low_ref, (rows, pl.ds(LANES, LANES)), im * c - re * s)
 
 
-def inverse_blocks(source, mid, out, half, twiddle, feature_q, skipped):
+def inverse_blocks(source, mid, out, half, twiddle, feature_q, gains, g_all):
     for f1 in range(4):
         values = []
         for f2 in range(8):
@@ -128,6 +128,7 @@
             re, im = times(spectrum[k2], 2 * np.pi * k2 * (0.25 + f1) / 32)
             mid[0, f1, k2] = re
             mid[1, f1, k2] = im
+    gain = gains[...]
     for k2 in range(8):
         u = fft4([(mid[0, f1, k2], mid[1, f1, k2]) for f1 in range(4)], 1)
         for k1 in range(4):
@@ -135,7 +136,7 @@
             re, im = u[k1]
             y = re if k1 == 0 else re * float(np.cos(angle)) - im * float(np.sin(angle))
             k = k2 + 8 * k1
-            out[half, k] = (feature_q[k] * (y + skipped[k])).astype(BF16)
+            out[half, k] = (feature_q[k] * (y + gain * g_all[half, k].astype(F32))).astype(BF16)
 
 
 def dot(a, b):
@@ -176,7 +177,7 @@
     q_hbm, k_hbm, v_hbm, fw_hbm, h_hbm, skip_hbm, w_hbm, tw_hbm, dft_hbm,
     out_ref,
     q_in, k_in, v_in, fw_ref, h_in, skip_ref, w_in, twiddle, dft,
-    tails, halo, extended, columns, feature_q, skipped,
+    tails, halo, extended, columns, feature_q, gains,
     h_send, g_send, q_send, m_send, h_all, g_all, q_all,
     mid, high_ref, low_ref, h_spec, v_spec, mixed, total, out_stage,
     local_sem, halo_sem, h_sem, g_sem, q_sem, m_sem, swap_sem, out_sem,
@@ -309,14 +310,14 @@
 
     def query_features(part):
         own = columns[pl.ds(pl.multiple_of(part * WIDTH + me * ROWS, ROWS), ROWS), :]
-        gain, w0, w1, w2 = [jnp.broadcast_to(own[:, i : i + 1], (ROWS, LANES)) for i in range(4)]
+        w0, w1, w2 = [jnp.broadcast_to(own[:, i : i + 1], (ROWS, LANES)) for i in range(1, 4)]
+        gains[...] = jnp.broadcast_to(own[:, 0:1], (ROWS, LANES))
         before1 = before2 = jnp.zeros((ROWS, LANES), F32)
         for k in range(BLOCKS):
             x = q_all[part, k].astype(F32)
             now1, now2 = pltpu.roll(x, 1, 1), pltpu.roll(x, 2, 1)
             shifted = w1 * jnp.where(lane < 1, before1, now1) + w2 * jnp.where(lane < 2, before2, now2)
             feature_q[k] = w0 * x + shifted
-            skipped[k] = gain * g_all[part, k].astype(F32)
             before1, before2 = now1, now2
 
     def convolve(part, carry):
@@ -325,7 +326,7 @@
         multiply_spectra(high_ref, low_ref, dft, h_spec, part, v_spec)
         all_of(q_all, part, q_sem).wait_recv()
         query_features(part)
-        inverse_blocks(v_spec, mid, m_send, part, twiddle, feature_q, skipped)
+        inverse_blocks(v_spec, mid, m_send, part, twiddle, feature_q, gains, g_all)
         for side, target in ((1, across), (0, mine)):
             for peer in peers + [me] * side:
                 pltpu.make_async_remote_copy(
@@ -357,7 +358,7 @@
         return dot(tokens, w_in[rows, cols])
 
     def by_token(slot, part):
-        return mixed[slot, part].reshape(WIDTH, LANES).astype(F32).T.astype(BF16)
+        return mixed[slot, part].reshape(WIDTH, LANES).T
 
     def project(slot, part):
         tokens = by_token(slot, part)
@@ -375,12 +376,12 @@
         arrived(0, part).wait_recv()
         swap(mine, 0, part).start()
         project(mine, part)
+        swap(diagonal, 1, part).wait_recv()
+        project(diagonal, part)
         swap(beside, 0, part).wait_recv()
-        project(beside, part)
-        swap(diagonal, 1, part).wait_recv()
         if part < PARTS - 1:
-            project(diagonal, part)
-    tokens = by_token(diagonal, PARTS - 1)
+            project(beside, part)
+    tokens = by_token(beside, PARTS - 1)
 
     def finish(j):
         cols = pl.ds(j * 256, 256)
@@ -388,7 +389,7 @@
 
     for j in range(4):
         cols = pl.ds(j * 256, 256)
-        out_stage[:, cols] = (total[:, cols] + product(tokens, diagonal, PARTS - 1, cols)).astype(BF16)
+        out_stage[:, cols] = (total[:, cols] + product(tokens, beside, PARTS - 1, cols)).astype(BF16)
         finish(j).start()
 
     for part in range(PARTS):
@@ -428,7 +429,7 @@
             pltpu.VMEM((2, tokens + 8, channels), F32),
             pltpu.VMEM((channels, 8), F32),
             pltpu.VMEM((BLOCKS, ROWS, LANES), F32),
-            pltpu.VMEM((BLOCKS, ROWS, LANES), F32),
+            pltpu.VMEM((ROWS, LANES), F32),
             pltpu.VMEM(turned, BF16),
             pltpu.VMEM(turned, BF16),
             pltpu.VMEM(turned, BF16),

time: 34.2 us -> 33.9 us (level)
  no operation moved by 1% of the time
where the time goes in v5:
time: 33.9 us; the launch traced here: 33.8 us
  Pallas kernels  32.1 us (95%)
  local copies, waits for them, and re-layouts  1.67 us (5%)
    pallas_call x1, Pallas kernels, shards(): pl.pallas_call(kernel, out_shape=jax.ShapeDtypeStruct((tokens, channels),...  32.1 us
    unnamed x1, local copies, waits for them, and re-layouts  1.67 us

profile of v5, /device:TPU:1, one launch (start us, length us, event | category | flops | bytes accessed | tf_op | source)
XLA Modules:
  0.0 33.8 jit_solution(10105910466342842637)
XLA Ops:
  0.0 32.1 %mixer.1 = bf16[128,1024]{1,0:T(8,128)(2,1)} custom-call(bf16[128,1024]{1,0:T(8,128)(2,1)} %q_hbm.1, bf16[128,1024]{1,0:T(8,128)(2,1)} %k_hbm.1, bf16[128,1024]{1,0:T(8,128)(2,1)} %v_hbm.1, f32[3,3,1024]{2,1,0:T(4,128)} %fw_hbm.1, f32[128,1024]{1,0:T(8,128)} %h_hbm.1, f32[1,1024]{1,0:T(1,128)} %bitcast.1, bf16[4096,1024]{1,0:T(8,128)(2,1)} %w_hbm.1, ...), custom_call_target="tpu_custom_call" | custom-call | tf_op jit(solution)/shard_map/mixer/pallas_call | solution.py:412
  32.1 1.7 %copy.11 = bf16[128,1024]{1,0:T(8,128)(2,1)} copy(bf16[128,1024]{1,0:T(8,128)(2,1)} %mixer.1) | data formatting | bytes 524288

commit v6 on v5

--- a/solution.py
+++ b/solution.py
@@ -287,13 +287,10 @@
         g_send[part, blocks] = turned(feature(0, cols) * feature(1, cols))
         return carry
 
-    def gate_part(part, carry):
-        lax.fori_loop(part * (8 // PARTS), (part + 1) * (8 // PARTS), gate, 0)
+    for part in range(PARTS):
+        lax.fori_loop(part * (8 // PARTS), (part + 1) * (8 // PARTS), gate, 0, unroll=True)
         scatter(g_send, g_all, part, g_sem)
         scatter(q_send, q_all, part, q_sem)
-        return carry
-
-    lax.fori_loop(0, PARTS, gate_part, 0)
 
     local[6].wait()
     local[7].wait()

time: 33.9 us -> 33.6 us (level)
  no operation moved by 1% of the time
where the time goes in v6:
time: 33.6 us; the launch traced here: 33.5 us
  Pallas kernels  31.8 us (95%)
  local copies, waits for them, and re-layouts  1.67 us (5%)
    pallas_call x1, Pallas kernels, shards(): pl.pallas_call(kernel, out_shape=jax.ShapeDtypeStruct((tokens, channels),...  31.8 us
    unnamed x1, local copies, waits for them, and re-layouts  1.67 us

profile of v6, /device:TPU:1, one launch (start us, length us, event | category | flops | bytes accessed | tf_op | source)
XLA Modules:
  0.0 33.5 jit_solution(11077538759960802637)
XLA Ops:
  0.0 31.8 %mixer.1 = bf16[128,1024]{1,0:T(8,128)(2,1)} custom-call(bf16[128,1024]{1,0:T(8,128)(2,1)} %q_hbm.1, bf16[128,1024]{1,0:T(8,128)(2,1)} %k_hbm.1, bf16[128,1024]{1,0:T(8,128)(2,1)} %v_hbm.1, f32[3,3,1024]{2,1,0:T(4,128)} %fw_hbm.1, f32[128,1024]{1,0:T(8,128)} %h_hbm.1, f32[1,1024]{1,0:T(1,128)} %bitcast.1, bf16[4096,1024]{1,0:T(8,128)(2,1)} %w_hbm.1, ...), custom_call_target="tpu_custom_call" | custom-call | tf_op jit(solution)/shard_map/mixer/pallas_call | solution.py:409
  31.8 1.7 %copy.11 = bf16[128,1024]{1,0:T(8,128)(2,1)} copy(bf16[128,1024]{1,0:T(8,128)(2,1)} %mixer.1) | data formatting | bytes 524288
